TPU v7x, 32 devices: a whole 2x2x4 slice. The times are simulated.
32 devices in a mesh: depth: 2 (over x), tx: 4 (over y, core), ty: 4 (over z).
Axes of the slice: x: 2, y: 2, z: 4, core: 2. Of those that a mesh axis runs over, the one named last changes fastest.
Arguments:
- volume: float32 [32, 1024, 512], P('depth', 'tx', 'ty'), may hold values from -6 to 6
- centers: float32 [4], replicated, may hold values from -1.5 to 1.5
- widths: float32 [4], replicated, may hold values from 0.3 to 1
- density: float32 [4], replicated, may hold values from 0.5 to 6
- colors: float32 [3, 4], replicated, may hold values from 0.05 to 1
Outputs:
- image: float32 [4, 1024, 512], P(None, ('tx', 'depth'), 'ty')
All inputs are finite; a program needn't handle non-finite values.
Results may differ from a plain program's by a relative error of at most 0.0001.
Values sent between devices are 32-bit elements; how exact they have to be, the bound alone decides.
No kernel may reach another device: no remote copies, remote signals or barrier semaphores. Data moves between devices by JAX's collectives and lax.ppermute only.
A program may use at most 64 MiB of HBM per device.

v0:
```python
import jax
import jax.numpy as jnp
from jax import lax
from jax.sharding import PartitionSpec as P

LIGHT_X = 0.36
LIGHT_Y = 0.48
LIGHT_Z = 0.8


def padded_2(cells, sides, width):
    for axis, dim in sides:
        count = lax.axis_size(axis)
        ends = count - 1
        head = lax.slice_in_dim(cells, 0, width, axis=dim)
        tail = lax.slice_in_dim(cells, cells.shape[dim] - width, cells.shape[dim], axis=dim)
        cells = jnp.concatenate(
            [
                lax.ppermute(tail, axis, [(i, (i + 1) % count) for i in range(ends)]),
                cells,
                lax.ppermute(head, axis, [((i + 1) % count, i) for i in range(ends)]),
            ],
            axis=dim,
        )
    return cells


def carried_in(part, axis, combine, identity):
    place = lax.axis_index(axis)
    gathered = lax.all_gather(part, axis)
    state = jnp.zeros_like(part) + jnp.asarray(identity, part.dtype)

    def one(hop, state):
        return combine(state, lax.dynamic_index_in_dim(gathered, hop, 0, False))

    return lax.fori_loop(0, place, one, state)


def composite(colour, trans, before, current, after, centers, widths, density, colors, step_len):
    middle = current[1:-1, 1:-1]
    grad_x = (current[2:, 1:-1] - current[:-2, 1:-1]) * 0.5
    grad_y = (current[1:-1, 2:] - current[1:-1, :-2]) * 0.5
    grad_z = (after - before) * 0.5
    grad_sq = grad_x * grad_x + grad_y * grad_y + grad_z * grad_z
    facing = jnp.abs(grad_x * LIGHT_X + grad_y * LIGHT_Y + grad_z * LIGHT_Z) * lax.rsqrt(
        grad_sq + 1.0
    )
    shade = 0.2 + 0.8 * facing
    scaled = (middle[None] - centers[:, None, None]) / widths[:, None, None]
    bumps = jnp.exp(-scaled * scaled)
    sigma = jnp.sum(density[:, None, None] * bumps, 0) * (1.0 - 0.8 / (1.0 + grad_sq))
    tint = jnp.sum(colors[:, :, None, None] * bumps[None], 1)
    shaded = shade[None] * tint / (1.0 + jnp.sum(bumps, 0))[None]
    passed = jnp.exp(-sigma * step_len)
    colour = colour + (trans * (1.0 - passed))[None] * shaded
    trans = trans * passed
    return (colour, trans)


def multiply(earlier, later):
    return earlier * later


def on_device(volume, centers, widths, density, colors):
    slices = volume.shape[0]
    tile_rows = volume.shape[1]
    tile_cols = volume.shape[2]
    depth_count = lax.axis_size("depth")
    step_len = 1.0 / (slices * depth_count)
    padded = padded_2(volume, (("depth", 0), ("tx", 1), ("ty", 2)), 1)

    def advance(index, state_pair):
        colour, trans = state_pair
        before = lax.dynamic_index_in_dim(padded, index, 0, keepdims=False)[1:-1, 1:-1]
        current = lax.dynamic_index_in_dim(padded, index + 1, 0, keepdims=False)
        after = lax.dynamic_index_in_dim(padded, index + 2, 0, keepdims=False)[1:-1, 1:-1]
        return composite(
            colour, trans, before, current, after, centers, widths, density, colors, step_len
        )

    start = (
        jnp.zeros((3, tile_rows, tile_cols), jnp.float32),
        jnp.ones((tile_rows, tile_cols), jnp.float32),
    )
    colour, trans = lax.fori_loop(0, slices, advance, start)
    front = carried_in(trans, "depth", multiply, jnp.ones_like(trans))
    terms = jnp.concatenate([front[None] * colour, (front * (1.0 - trans))[None]], 0)
    return lax.psum_scatter(terms, "depth", scatter_dimension=1, tiled=True)


def solution(mesh):
    return jax.shard_map(
        on_device,
        mesh=mesh,
        in_specs=(P("depth", "tx", "ty"), P(), P(), P(), P()),
        out_specs=P(None, ("tx", "depth"), "ty"),
        check_vma=False,
    )
```

profile of v0, /device:TPU:0, one launch (start us, length us, event | category | flops | bytes accessed | tf_op | source)
XLA Modules:
  0.0 115.4 jit_solution(14287535974557454584)
XLA Ops:
  6.5 1.0 fusion.4
  7.5 4.9 %collective-permute-start = (f32[1,256,128]{2,1,0:T(8,128)S(1)}, f32[1,256,128]{2,1,0:T(8,128)S(1)}, u32[]{:S(2)}, u32[]{:S(2)}) collective-permute-start(f32[1,256,128]{2,1,0:T(8,128)S(1)} %get-tuple-element.308), channel_id=1, source_target_pairs={{0,16},{1,17},{2,18},{3,19},{4,20},{5,21},{6,22},{7,23},{8,24},{9,... | collective-permute-start | bytes 393224 | tf_op jit(solution)/shard_map/ppermute | solution.py:19
  12.4 1.3 %collective-permute-start.1 = (f32[1,256,128]{2,1,0:T(8,128)S(1)}, f32[1,256,128]{2,1,0:T(8,128)S(1)}, u32[]{:S(2)}, u32[]{:S(2)}) collective-permute-start(f32[1,256,128]{2,1,0:T(8,128)S(1)} %get-tuple-element.307), channel_id=1, source_target_pairs={{16,0},{17,1},{18,2},{19,3},{20,4},{21,5},{22,6},{23,7},{24,8},{25... | collective-permute-start | bytes 393224 | tf_op jit(solution)/shard_map/ppermute | solution.py:21
  13.7 1.4 %collective-permute-done = f32[1,256,128]{2,1,0:T(8,128)S(1)} collective-permute-done((f32[1,256,128]{2,1,0:T(8,128)S(1)}, f32[1,256,128]{2,1,0:T(8,128)S(1)}, u32[]{:S(2)}, u32[]{:S(2)}) %collective-permute-start) | collective-permute-done | bytes 131104 | tf_op jit(solution)/shard_map/ppermute | solution.py:19
  15.2 1.7 %constant_dynamic-update-slice_fusion.1 = f32[18,256,128]{2,1,0:T(8,128)S(1)} fusion(f32[18,256,128]{2,1,0:T(8,128)S(1)} %constant_dynamic-update-slice_fusion.2, f32[16,256,128]{2,1,0:T(8,128)} %param.9), kind=kLoop, calls=%fused_computation.25 | loop fusion | bytes 4194304
  16.9 2.4 %collective-permute-done.1 = f32[1,256,128]{2,1,0:T(8,128)S(1)} collective-permute-done((f32[1,256,128]{2,1,0:T(8,128)S(1)}, f32[1,256,128]{2,1,0:T(8,128)S(1)}, u32[]{:S(2)}, u32[]{:S(2)}) %collective-permute-start.1) | collective-permute-done | bytes 131104 | tf_op jit(solution)/shard_map/ppermute | solution.py:21
  19.3 1.3 %collective-permute-start.2 = (f32[18,1,128]{2,1,0:T(1,128)S(1)}, f32[18,1,128]{2,1,0:T(1,128)S(1)}, u32[]{:S(2)}, u32[]{:S(2)}) collective-permute-start(f32[18,1,128]{2,1,0:T(1,128)S(1)} %get-tuple-element.305), channel_id=1, source_target_pairs={{0,4},{4,8},{8,12},{1,5},{5,9},{9,13},{2,6},{6,10},{10,14},{3,7},{... | collective-permute-start | bytes 27656 | tf_op jit(solution)/shard_map/ppermute | solution.py:19
  20.6 1.3 %collective-permute-start.3 = (f32[18,1,128]{2,1,0:T(1,128)S(1)}, f32[18,1,128]{2,1,0:T(1,128)S(1)}, u32[]{:S(2)}, u32[]{:S(2)}) collective-permute-start(f32[18,1,128]{2,1,0:T(1,128)S(1)} %get-tuple-element.306), channel_id=1, source_target_pairs={{4,0},{8,4},{12,8},{5,1},{9,5},{13,9},{6,2},{10,6},{14,10},{7,3},{... | collective-permute-start | bytes 27656 | tf_op jit(solution)/shard_map/ppermute | solution.py:21
  21.9 3.5 %collective-permute-done.3 = f32[18,1,128]{2,1,0:T(1,128)S(1)} collective-permute-done((f32[18,1,128]{2,1,0:T(1,128)S(1)}, f32[18,1,128]{2,1,0:T(1,128)S(1)}, u32[]{:S(2)}, u32[]{:S(2)}) %collective-permute-start.3) | collective-permute-done | bytes 9248 | tf_op jit(solution)/shard_map/ppermute | solution.py:21
  25.6 2.9 %fusion.2 = (f32[18,258,1]{2,1,0:T(8,128)}, f32[18,258,1]{2,1,0:T(8,128)}) fusion(f32[18,258,128]{2,1,0:T(8,128)S(1)} %pad_maximum_fusion.1), kind=kLoop, calls=%fused_computation.27 | loop fusion | bytes 74304 | tf_op jit(solution)/shard_map/slice | solution.py:16
  28.5 2.7 %copy.14 = f32[18,258,1]{1,2,0:T(1,128)S(1)} copy(f32[18,258,1]{2,1,0:T(8,128)} %get-tuple-element.303) | data formatting | bytes 37152 | tf_op jit(solution)/shard_map/slice | solution.py:16
  31.2 3.5 %collective-permute-start.4 = (f32[18,258,1]{1,2,0:T(1,128)S(1)}, f32[18,258,1]{1,2,0:T(1,128)S(1)}, u32[]{:S(2)}, u32[]{:S(2)}) collective-permute-start(f32[18,258,1]{1,2,0:T(1,128)S(1)} %copy.14), channel_id=1, source_target_pairs={{0,1},{1,2},{2,3},{4,5},{5,6},{6,7},{8,9},{9,10},{10,11},{12,13},{... | collective-permute-start | bytes 55736 | tf_op jit(solution)/shard_map/ppermute | solution.py:19
  34.7 2.7 %copy.15 = f32[18,258,1]{1,2,0:T(1,128)S(1)} copy(f32[18,258,1]{2,1,0:T(8,128)} %get-tuple-element.304) | data formatting | bytes 37152 | tf_op jit(solution)/shard_map/slice | solution.py:15
  37.4 1.3 %collective-permute-start.5 = (f32[18,258,1]{1,2,0:T(1,128)S(1)}, f32[18,258,1]{1,2,0:T(1,128)S(1)}, u32[]{:S(2)}, u32[]{:S(2)}) collective-permute-start(f32[18,258,1]{1,2,0:T(1,128)S(1)} %copy.15), channel_id=1, source_target_pairs={{1,0},{2,1},{3,2},{5,4},{6,5},{7,6},{9,8},{10,9},{11,10},{13,12},{... | collective-permute-start | bytes 55736 | tf_op jit(solution)/shard_map/ppermute | solution.py:21
  38.8 2.3 %copy.16 = f32[18,258,1]{2,1,0:T(8,128)} copy(f32[18,258,1]{1,2,0:T(1,128)S(1)} %collective-permute-done.4) | data formatting | bytes 37152 | tf_op jit(solution)/shard_map/ppermute | solution.py:19
  41.1 2.1 %collective-permute-done.5 = f32[18,258,1]{1,2,0:T(1,128)S(1)} collective-permute-done((f32[18,258,1]{1,2,0:T(1,128)S(1)}, f32[18,258,1]{1,2,0:T(1,128)S(1)}, u32[]{:S(2)}, u32[]{:S(2)}) %collective-permute-start.5) | collective-permute-done | bytes 18608 | tf_op jit(solution)/shard_map/ppermute | solution.py:21
  43.2 2.3 %copy.17 = f32[18,258,1]{2,1,0:T(8,128)} copy(f32[18,258,1]{1,2,0:T(1,128)S(1)} %collective-permute-done.5) | data formatting | bytes 37152 | tf_op jit(solution)/shard_map/ppermute | solution.py:21
  45.5 6.2 %pad_maximum_fusion = f32[18,258,130]{2,1,0:T(8,128)} fusion(f32[18,258,1]{2,1,0:T(8,128)} %copy.17, f32[18,1,128]{2,1,0:T(1,128)S(1)} %collective-permute-done.3, f32[18,256,128]{2,1,0:T(8,128)S(1)} %constant_dynamic-update-slice_fusion, f32[18,1,128]{2,1,0:T(1,128)S(1)} %collective-permute-done.2, f32[18,258,1]{2,1,0:T(8,128)} %copy.16), kind=kLoop, calls=%fused_computation.19 | loop fusion | flops 2414880 | bytes 4829760 | tf_op jit(solution)/shard_map/concatenate | solution.py:17
  51.6 35.4 %while.29 = (s32[]{:T(128)}, f32[3,256,128]{2,1,0:T(8,128)S(1)}, f32[256,128]{1,0:T(8,128)S(1)}, f32[4]{0:T(128)S(1)}, f32[18,258,130]{2,1,0:T(8,128)}, /*index=...) while((s32[]{:T(128)}, f32[3,256,128]{2,1,0:T(8,128)S(1)}, ...), condition=%wide.region_4.5_spmd.clone, body=%wide.region_0.4_spmd.clone.sunk | while | flops 3080202 | bytes 6834605 | solution.py:85
  51.7 1.2 %dynamic-slice_bitcast_fusion.4 = (f32[258,130]{1,0:T(8,128)S(1)}, f32[258,130]{1,0:T(8,128)S(1)}, f32[258,130]{1,0:T(8,128)S(1)}) fusion(f32[18,258,130]{2,1,0:T(8,128)} %get-tuple-element.434, s32[]{:T(128)S(6)} %select_n.40, s32[]{:T(128)} %get-tuple-element.417, s32[]{:T(128)S(6)} %select_n.41), kind=kLoop, calls=%fused_computation.7.clone.1 | loop fusion | bytes 804972 | tf_op jit(solution)/shard_map/while/body/eval_jaxpr/jit(dynamic_index_in_dim)/squeeze | solution.py:76
  53.0 0.2 multiply_reduce_fusion.4
  53.2 0.3 select_multiply_fusion.2
  53.9 1.2 %dynamic-slice_bitcast_fusion.4 = (f32[258,130]{1,0:T(8,128)S(1)}, f32[258,130]{1,0:T(8,128)S(1)}, f32[258,130]{1,0:T(8,128)S(1)}) fusion(f32[18,258,130]{2,1,0:T(8,128)} %get-tuple-element.434, s32[]{:T(128)S(6)} %select_n.40, s32[]{:T(128)} %get-tuple-element.417, s32[]{:T(128)S(6)} %select_n.41), kind=kLoop, calls=%fused_computation.7.clone.1 | loop fusion | bytes 804972 | tf_op jit(solution)/shard_map/while/body/eval_jaxpr/jit(dynamic_index_in_dim)/squeeze | solution.py:76
  55.2 0.2 multiply_reduce_fusion.4
  55.4 0.3 select_multiply_fusion.2
  56.1 1.2 %dynamic-slice_bitcast_fusion.4 = (f32[258,130]{1,0:T(8,128)S(1)}, f32[258,130]{1,0:T(8,128)S(1)}, f32[258,130]{1,0:T(8,128)S(1)}) fusion(f32[18,258,130]{2,1,0:T(8,128)} %get-tuple-element.434, s32[]{:T(128)S(6)} %select_n.40, s32[]{:T(128)} %get-tuple-element.417, s32[]{:T(128)S(6)} %select_n.41), kind=kLoop, calls=%fused_computation.7.clone.1 | loop fusion | bytes 804972 | tf_op jit(solution)/shard_map/while/body/eval_jaxpr/jit(dynamic_index_in_dim)/squeeze | solution.py:76
  57.4 0.2 multiply_reduce_fusion.4
  57.7 0.3 select_multiply_fusion.2
  58.3 1.2 %dynamic-slice_bitcast_fusion.4 = (f32[258,130]{1,0:T(8,128)S(1)}, f32[258,130]{1,0:T(8,128)S(1)}, f32[258,130]{1,0:T(8,128)S(1)}) fusion(f32[18,258,130]{2,1,0:T(8,128)} %get-tuple-element.434, s32[]{:T(128)S(6)} %select_n.40, s32[]{:T(128)} %get-tuple-element.417, s32[]{:T(128)S(6)} %select_n.41), kind=kLoop, calls=%fused_computation.7.clone.1 | loop fusion | bytes 804972 | tf_op jit(solution)/shard_map/while/body/eval_jaxpr/jit(dynamic_index_in_dim)/squeeze | solution.py:76
  59.6 0.2 multiply_reduce_fusion.4
  59.9 0.3 select_multiply_fusion.2
  60.5 1.2 %dynamic-slice_bitcast_fusion.4 = (f32[258,130]{1,0:T(8,128)S(1)}, f32[258,130]{1,0:T(8,128)S(1)}, f32[258,130]{1,0:T(8,128)S(1)}) fusion(f32[18,258,130]{2,1,0:T(8,128)} %get-tuple-element.434, s32[]{:T(128)S(6)} %select_n.40, s32[]{:T(128)} %get-tuple-element.417, s32[]{:T(128)S(6)} %select_n.41), kind=kLoop, calls=%fused_computation.7.clone.1 | loop fusion | bytes 804972 | tf_op jit(solution)/shard_map/while/body/eval_jaxpr/jit(dynamic_index_in_dim)/squeeze | solution.py:76
  61.8 0.2 multiply_reduce_fusion.4
  62.1 0.3 select_multiply_fusion.2
  62.7 1.2 %dynamic-slice_bitcast_fusion.4 = (f32[258,130]{1,0:T(8,128)S(1)}, f32[258,130]{1,0:T(8,128)S(1)}, f32[258,130]{1,0:T(8,128)S(1)}) fusion(f32[18,258,130]{2,1,0:T(8,128)} %get-tuple-element.434, s32[]{:T(128)S(6)} %select_n.40, s32[]{:T(128)} %get-tuple-element.417, s32[]{:T(128)S(6)} %select_n.41), kind=kLoop, calls=%fused_computation.7.clone.1 | loop fusion | bytes 804972 | tf_op jit(solution)/shard_map/while/body/eval_jaxpr/jit(dynamic_index_in_dim)/squeeze | solution.py:76
  64.0 0.2 multiply_reduce_fusion.4
  64.3 0.3 select_multiply_fusion.2
  65.0 1.2 %dynamic-slice_bitcast_fusion.4 = (f32[258,130]{1,0:T(8,128)S(1)}, f32[258,130]{1,0:T(8,128)S(1)}, f32[258,130]{1,0:T(8,128)S(1)}) fusion(f32[18,258,130]{2,1,0:T(8,128)} %get-tuple-element.434, s32[]{:T(128)S(6)} %select_n.40, s32[]{:T(128)} %get-tuple-element.417, s32[]{:T(128)S(6)} %select_n.41), kind=kLoop, calls=%fused_computation.7.clone.1 | loop fusion | bytes 804972 | tf_op jit(solution)/shard_map/while/body/eval_jaxpr/jit(dynamic_index_in_dim)/squeeze | solution.py:76
  66.3 0.2 multiply_reduce_fusion.4
  66.5 0.3 select_multiply_fusion.2
  67.2 1.2 %dynamic-slice_bitcast_fusion.4 = (f32[258,130]{1,0:T(8,128)S(1)}, f32[258,130]{1,0:T(8,128)S(1)}, f32[258,130]{1,0:T(8,128)S(1)}) fusion(f32[18,258,130]{2,1,0:T(8,128)} %get-tuple-element.434, s32[]{:T(128)S(6)} %select_n.40, s32[]{:T(128)} %get-tuple-element.417, s32[]{:T(128)S(6)} %select_n.41), kind=kLoop, calls=%fused_computation.7.clone.1 | loop fusion | bytes 804972 | tf_op jit(solution)/shard_map/while/body/eval_jaxpr/jit(dynamic_index_in_dim)/squeeze | solution.py:76
  68.5 0.2 multiply_reduce_fusion.4
  68.7 0.3 select_multiply_fusion.2
  69.4 1.2 %dynamic-slice_bitcast_fusion.4 = (f32[258,130]{1,0:T(8,128)S(1)}, f32[258,130]{1,0:T(8,128)S(1)}, f32[258,130]{1,0:T(8,128)S(1)}) fusion(f32[18,258,130]{2,1,0:T(8,128)} %get-tuple-element.434, s32[]{:T(128)S(6)} %select_n.40, s32[]{:T(128)} %get-tuple-element.417, s32[]{:T(128)S(6)} %select_n.41), kind=kLoop, calls=%fused_computation.7.clone.1 | loop fusion | bytes 804972 | tf_op jit(solution)/shard_map/while/body/eval_jaxpr/jit(dynamic_index_in_dim)/squeeze | solution.py:76
  70.9 0.3 select_multiply_fusion.2
  71.6 1.2 %dynamic-slice_bitcast_fusion.4 = (f32[258,130]{1,0:T(8,128)S(1)}, f32[258,130]{1,0:T(8,128)S(1)}, f32[258,130]{1,0:T(8,128)S(1)}) fusion(f32[18,258,130]{2,1,0:T(8,128)} %get-tuple-element.434, s32[]{:T(128)S(6)} %select_n.40, s32[]{:T(128)} %get-tuple-element.417, s32[]{:T(128)S(6)} %select_n.41), kind=kLoop, calls=%fused_computation.7.clone.1 | loop fusion | bytes 804972 | tf_op jit(solution)/shard_map/while/body/eval_jaxpr/jit(dynamic_index_in_dim)/squeeze | solution.py:76
  73.1 0.3 select_multiply_fusion.2
  73.8 1.2 %dynamic-slice_bitcast_fusion.4 = (f32[258,130]{1,0:T(8,128)S(1)}, f32[258,130]{1,0:T(8,128)S(1)}, f32[258,130]{1,0:T(8,128)S(1)}) fusion(f32[18,258,130]{2,1,0:T(8,128)} %get-tuple-element.434, s32[]{:T(128)S(6)} %select_n.40, s32[]{:T(128)} %get-tuple-element.417, s32[]{:T(128)S(6)} %select_n.41), kind=kLoop, calls=%fused_computation.7.clone.1 | loop fusion | bytes 804972 | tf_op jit(solution)/shard_map/while/body/eval_jaxpr/jit(dynamic_index_in_dim)/squeeze | solution.py:76
  75.4 0.3 select_multiply_fusion.2
  76.0 1.2 %dynamic-slice_bitcast_fusion.4 = (f32[258,130]{1,0:T(8,128)S(1)}, f32[258,130]{1,0:T(8,128)S(1)}, f32[258,130]{1,0:T(8,128)S(1)}) fusion(f32[18,258,130]{2,1,0:T(8,128)} %get-tuple-element.434, s32[]{:T(128)S(6)} %select_n.40, s32[]{:T(128)} %get-tuple-element.417, s32[]{:T(128)S(6)} %select_n.41), kind=kLoop, calls=%fused_computation.7.clone.1 | loop fusion | bytes 804972 | tf_op jit(solution)/shard_map/while/body/eval_jaxpr/jit(dynamic_index_in_dim)/squeeze | solution.py:76
  77.3 0.2 multiply_reduce_fusion.4
  77.6 0.3 select_multiply_fusion.2
  78.2 1.2 %dynamic-slice_bitcast_fusion.4 = (f32[258,130]{1,0:T(8,128)S(1)}, f32[258,130]{1,0:T(8,128)S(1)}, f32[258,130]{1,0:T(8,128)S(1)}) fusion(f32[18,258,130]{2,1,0:T(8,128)} %get-tuple-element.434, s32[]{:T(128)S(6)} %select_n.40, s32[]{:T(128)} %get-tuple-element.417, s32[]{:T(128)S(6)} %select_n.41), kind=kLoop, calls=%fused_computation.7.clone.1 | loop fusion | bytes 804972 | tf_op jit(solution)/shard_map/while/body/eval_jaxpr/jit(dynamic_index_in_dim)/squeeze | solution.py:76
  79.8 0.3 select_multiply_fusion.2
  80.4 1.2 %dynamic-slice_bitcast_fusion.4 = (f32[258,130]{1,0:T(8,128)S(1)}, f32[258,130]{1,0:T(8,128)S(1)}, f32[258,130]{1,0:T(8,128)S(1)}) fusion(f32[18,258,130]{2,1,0:T(8,128)} %get-tuple-element.434, s32[]{:T(128)S(6)} %select_n.40, s32[]{:T(128)} %get-tuple-element.417, s32[]{:T(128)S(6)} %select_n.41), kind=kLoop, calls=%fused_computation.7.clone.1 | loop fusion | bytes 804972 | tf_op jit(solution)/shard_map/while/body/eval_jaxpr/jit(dynamic_index_in_dim)/squeeze | solution.py:76
  82.0 0.3 select_multiply_fusion.2
  82.7 1.2 %dynamic-slice_bitcast_fusion.4 = (f32[258,130]{1,0:T(8,128)S(1)}, f32[258,130]{1,0:T(8,128)S(1)}, f32[258,130]{1,0:T(8,128)S(1)}) fusion(f32[18,258,130]{2,1,0:T(8,128)} %get-tuple-element.434, s32[]{:T(128)S(6)} %select_n.40, s32[]{:T(128)} %get-tuple-element.417, s32[]{:T(128)S(6)} %select_n.41), kind=kLoop, calls=%fused_computation.7.clone.1 | loop fusion | bytes 804972 | tf_op jit(solution)/shard_map/while/body/eval_jaxpr/jit(dynamic_index_in_dim)/squeeze | solution.py:76
  84.2 0.3 select_multiply_fusion.2
  84.9 1.2 %dynamic-slice_bitcast_fusion.4 = (f32[258,130]{1,0:T(8,128)S(1)}, f32[258,130]{1,0:T(8,128)S(1)}, f32[258,130]{1,0:T(8,128)S(1)}) fusion(f32[18,258,130]{2,1,0:T(8,128)} %get-tuple-element.434, s32[]{:T(128)S(6)} %select_n.40, s32[]{:T(128)} %get-tuple-element.417, s32[]{:T(128)S(6)} %select_n.41), kind=kLoop, calls=%fused_computation.7.clone.1 | loop fusion | bytes 804972 | tf_op jit(solution)/shard_map/while/body/eval_jaxpr/jit(dynamic_index_in_dim)/squeeze | solution.py:76
  86.2 0.2 multiply_reduce_fusion.4
  86.4 0.3 select_multiply_fusion.2
  87.1 7.0 %all-gather = f32[512,128]{1,0:T(8,128)S(1)} all-gather(f32[256,128]{1,0:T(8,128)S(1)} %get-tuple-element.231), channel_id=2, replica_groups=mesh['depth'=2,'tx'=4,'ty'=4] {'depth'}, dimensions={0}, use_global_device_ids=true | all-gather | bytes 393216 | tf_op jit(solution)/shard_map/all_gather | solution.py:30
  94.2 0.8 pad_maximum_fusion.2
  95.1 13.5 %reduce-scatter.2.cloned.1.call-done = f32[4,128,128]{2,1,0:T(8,128)} async-done(((f32[4,256,128]{2,1,0:T(8,128)}), f32[4,128,128]{2,1,0:T(8,128)}) %reduce-scatter.2.cloned.1.call-update) | async-done | bytes 262160 | tf_op jit(solution)/shard_map/reduce_scatter | solution.py:88
  (108 shorter events, 8.5 us)
Async XLA Ops:
  6.5 102.0 %reduce-scatter.2.cloned.1.call-start = ((), (), s32[]{:S(2)}) async-start(), calls=%async_computation.1 | async-start | bytes 786432 | tf_op jit(solution)/shard_map/reduce_scatter | solution.py:88
  7.5 7.6 %collective-permute-start = (f32[1,256,128]{2,1,0:T(8,128)S(1)}, f32[1,256,128]{2,1,0:T(8,128)S(1)}, u32[]{:S(2)}, u32[]{:S(2)}) collective-permute-start(f32[1,256,128]{2,1,0:T(8,128)S(1)} %get-tuple-element.308), channel_id=1, source_target_pairs={{0,16},{1,17},{2,18},{3,19},{4,20},{5,21},{6,22},{7,23},{8,24},{9,... | collective-permute-start | bytes 393224 | tf_op jit(solution)/shard_map/ppermute | solution.py:19
  12.4 6.9 %collective-permute-start.1 = (f32[1,256,128]{2,1,0:T(8,128)S(1)}, f32[1,256,128]{2,1,0:T(8,128)S(1)}, u32[]{:S(2)}, u32[]{:S(2)}) collective-permute-start(f32[1,256,128]{2,1,0:T(8,128)S(1)} %get-tuple-element.307), channel_id=1, source_target_pairs={{16,0},{17,1},{18,2},{19,3},{20,4},{21,5},{22,6},{23,7},{24,8},{25... | collective-permute-start | bytes 393224 | tf_op jit(solution)/shard_map/ppermute | solution.py:21
  19.3 2.6 %collective-permute-start.2 = (f32[18,1,128]{2,1,0:T(1,128)S(1)}, f32[18,1,128]{2,1,0:T(1,128)S(1)}, u32[]{:S(2)}, u32[]{:S(2)}) collective-permute-start(f32[18,1,128]{2,1,0:T(1,128)S(1)} %get-tuple-element.305), channel_id=1, source_target_pairs={{0,4},{4,8},{8,12},{1,5},{5,9},{9,13},{2,6},{6,10},{10,14},{3,7},{... | collective-permute-start | bytes 27656 | tf_op jit(solution)/shard_map/ppermute | solution.py:19
  20.6 4.8 %collective-permute-start.3 = (f32[18,1,128]{2,1,0:T(1,128)S(1)}, f32[18,1,128]{2,1,0:T(1,128)S(1)}, u32[]{:S(2)}, u32[]{:S(2)}) collective-permute-start(f32[18,1,128]{2,1,0:T(1,128)S(1)} %get-tuple-element.306), channel_id=1, source_target_pairs={{4,0},{8,4},{12,8},{5,1},{9,5},{13,9},{6,2},{10,6},{14,10},{7,3},{... | collective-permute-start | bytes 27656 | tf_op jit(solution)/shard_map/ppermute | solution.py:21
  31.2 7.5 %collective-permute-start.4 = (f32[18,258,1]{1,2,0:T(1,128)S(1)}, f32[18,258,1]{1,2,0:T(1,128)S(1)}, u32[]{:S(2)}, u32[]{:S(2)}) collective-permute-start(f32[18,258,1]{1,2,0:T(1,128)S(1)} %copy.14), channel_id=1, source_target_pairs={{0,1},{1,2},{2,3},{4,5},{5,6},{6,7},{8,9},{9,10},{10,11},{12,13},{... | collective-permute-start | bytes 55736 | tf_op jit(solution)/shard_map/ppermute | solution.py:19
  37.4 5.8 %collective-permute-start.5 = (f32[18,258,1]{1,2,0:T(1,128)S(1)}, f32[18,258,1]{1,2,0:T(1,128)S(1)}, u32[]{:S(2)}, u32[]{:S(2)}) collective-permute-start(f32[18,258,1]{1,2,0:T(1,128)S(1)} %copy.15), channel_id=1, source_target_pairs={{1,0},{2,1},{3,2},{5,4},{6,5},{7,6},{9,8},{10,9},{11,10},{13,12},{... | collective-permute-start | bytes 55736 | tf_op jit(solution)/shard_map/ppermute | solution.py:21
  45.4 6.2 %copy-start = (f32[3,4]{1,0:T(4,128)S(1)}, f32[3,4]{1,0:T(4,128)}, u32[]{:S(2)}) copy-start(f32[3,4]{1,0:T(4,128)} %param.13) | copy-start | bytes 148
  45.4 6.2 %copy-start.1 = (f32[4]{0:T(128)S(1)}, f32[4]{0:T(128)}, u32[]{:S(2)}) copy-start(f32[4]{0:T(128)} %param.12) | copy-start | bytes 52
  45.4 6.2 %copy-start.2 = (f32[4]{0:T(128)S(1)}, f32[4]{0:T(128)}, u32[]{:S(2)}) copy-start(f32[4]{0:T(128)} %param.10) | copy-start | bytes 52
  45.5 6.2 %copy-start.3 = (f32[4]{0:T(128)S(1)}, f32[4]{0:T(128)}, u32[]{:S(2)}) copy-start(f32[4]{0:T(128)} %param.11) | copy-start | bytes 52
Sparse Core Ops, SparseCore 0:
  95.2 13.3 reduce-scatter.1
where the time goes:
time: 116 us; the launch traced here: 115 us
  local copies, waits for them, and re-layouts  36.5 us (31%)
  waiting for transfers between devices  23 us (20%)
  other arithmetic  20.3 us (18%)
  between operations  13.6 us (12%)
  starting transfers between devices  13.5 us (12%)
  blocking collectives  7.03 us (6%)
  loops' own time  1.48 us (1%)
    squeeze x16, local copies, waits for them, and re-layouts, advance(): lax.dynamic_index_in_dim(padded, index + 2, 0, keepdims=False)[1:-1, 1:-1]  19.1 us
    reduce_scatter x1, waiting for transfers between devices, on_device(): return lax.psum_scatter(terms, 'depth', scatter_dimension=1, tiled=True)  13.5 us
    ppermute x3, starting transfers between devices, padded_2(): lax.ppermute(tail, axis, [(i, (i + 1) % count) for i in range(ends)])  9.65 us
    ppermute x3, waiting for transfers between devices, padded_2(): lax.ppermute(head, axis, [((i + 1) % count, i) for i in range(ends)])  7.99 us
    all_gather x1, blocking collectives, carried_in(): gathered = lax.all_gather(part, axis)  7.03 us
    concatenate x2, other arithmetic, padded_2(): jnp.concatenate([lax.ppermute(tail, axis, [(i, (i + 1) % count) for i in...  6.35 us
    slice x3, local copies, waits for them, and re-layouts, padded_2(): lax.slice_in_dim(cells, cells.shape[dim] - width, cells.shape[dim], axis=...  5.62 us
    mul x16, other arithmetic, composite(): trans = trans * passed  4.32 us
  transfers between devices with their start and end apart: 7, of which 5 were waited for; matrix products, arithmetic and copies ran while one was open for 6% of the time, Pallas kernels for 0%

commit v1 on v0

v1 whole, which is shorter than its diff:
```python
import functools
import math

import jax
import jax.numpy as jnp
from jax import lax
from jax.experimental import pallas as pl
from jax.experimental.pallas import tpu as pltpu
from jax.sharding import PartitionSpec as P

LIGHT_X = 0.36
LIGHT_Y = 0.48
LIGHT_Z = 0.8
AMBIENT = 0.2
PAD = 8
ROWS_AT_ONCE = 4
FRONT = ("centers", "widths", "density", "colors")

ANY = pl.BlockSpec(memory_space=pl.ANY)
VMEM = pl.BlockSpec(memory_space=pltpu.VMEM)
SMEM = pl.BlockSpec(memory_space=pltpu.SMEM)


def in_vmem(array):
    return pltpu.with_memory_space_constraint(array, pltpu.VMEM)


def vmem_out(*shape):
    return pltpu.VMEM(shape, jnp.float32)


def sends(low, high, even):
    return jnp.where(even, high, low), jnp.where(even, low, high)


def receives(first, second, place, count):
    even = place % 2 == 0
    low = jnp.where(even, second, first)
    high = jnp.where(even, first, second)
    return jnp.where(place > 0, low, 0.0), jnp.where(place < count - 1, high, 0.0)


def swap_rounds(axis, beside=None):
    count = lax.axis_size(axis)
    first = [(i, i ^ 1) for i in range(count)]
    inner = {i: (i + 1 if i % 2 else i - 1) for i in range(1, count - 1)}
    if beside is None or lax.axis_size(beside) % 2:
        second = [(i, inner.get(i, count - 1 - i)) for i in range(count)]
        return (axis, first), (axis, second)
    second = []
    for b in range(lax.axis_size(beside)):
        for i in range(count):
            to = (b, inner[i]) if i in inner else (b ^ 1, i)
            second.append((b * count + i, to[0] * count + to[1]))
    return (axis, first), ((beside, axis), second)


def pack_kernel(volume, padded, cols, col_a, col_b, row_a, row_b, depth_a, depth_b, packed, turned, sems):
    slices, rows, lanes = volume.shape

    def copy(s):
        return pltpu.make_async_copy(
            volume.at[s], padded.at[s, pl.ds(PAD, rows), :], sems.at[s]
        )

    for s in range(slices):
        copy(s).start()
    lane = lax.broadcasted_iota(jnp.int32, (rows, lanes), 1)
    packed[...] = jnp.zeros_like(packed)
    for s in range(slices):
        copy(s).wait()
        moved = pltpu.roll(padded[s, pl.ds(PAD, rows), :], 2 * s + 1, 1)
        packed[...] = jnp.where(lane // 2 == s, moved, packed[...])
    even_y = lax.axis_index("ty") % 2 == 0
    for h in range(rows // lanes):
        turned[h] = packed[pl.ds(h * lanes, lanes), :].T
        last = turned[h, pl.ds(0, slices, 2), :]
        first = turned[h, pl.ds(1, slices, 2), :]
        cols[0, h] = first
        cols[1, h] = last
        col_a[h], col_b[h] = sends(first, last, even_y)
    even_x = lax.axis_index("tx") % 2 == 0
    row_a[...], row_b[...] = sends(padded[:, PAD, :], padded[:, PAD + rows - 1, :], even_x)
    even_z = lax.axis_index("depth") % 2 == 0
    low = padded[0, pl.ds(PAD, rows), :]
    high = padded[slices - 1, pl.ds(PAD, rows), :]
    depth_a[...], depth_b[...] = sends(low, high, even_z)


def render(padded, edges, below, above, consts, outs, first_row, rows, step_len):
    centers, widths, density, colors = consts
    slices, _, lanes = padded.shape
    terms = centers.shape[0]
    tile = (8, lanes)
    log2e = math.log2(math.e)

    def splat(x):
        return jnp.full(tile, x, jnp.float32)

    beta = [splat(-log2e) / (splat(widths[k]) * splat(widths[k])) for k in range(terms)]
    thick = [splat(density[k]) * (-log2e * step_len) for k in range(terms)]
    centre = [splat(centers[k]) for k in range(terms)]
    lane = lax.broadcasted_iota(jnp.int32, tile, 1)
    edge = (lane == 0) | (lane == lanes - 1)
    zero, one = jnp.zeros(tile, jnp.float32), jnp.ones(tile, jnp.float32)

    def chunk(index, _):
        base = pl.multiple_of(first_row + index * (8 * ROWS_AT_ONCE), 8)
        for j in range(ROWS_AT_ONCE):
            row = pl.multiple_of(base + 8 * j, 8)
            edge_rows = edges[pl.ds(row, 8), :]
            total, trans = [zero] * terms, one
            before = below(row)
            current = padded[0, pl.ds(row + PAD, 8), :]
            for s in range(slices):
                after = padded[s + 1, pl.ds(row + PAD, 8), :] if s + 1 < slices else above(row)
                dx = padded[s, pl.ds(row + PAD + 1, 8), :] - padded[s, pl.ds(row + PAD - 1, 8), :]
                dy = pltpu.roll(current, lanes - 1, 1) - pltpu.roll(current, 1, 1)
                dy = dy + jnp.where(edge, pltpu.roll(edge_rows, lanes - (2 * s + 1), 1), 0.0)
                dz = after - before
                bumps = []
                for k in range(terms):
                    off = current - centre[k]
                    bumps.append(jnp.exp2(off * beta[k] * off))
                inv = lax.rsqrt((dx * dx + dy * dy) + (dz * dz + 4.0))
                lit = jnp.abs(dx * (LIGHT_X / LIGHT_Z) + dy * (LIGHT_Y / LIGHT_Z) + dz)
                shade = lit * inv + AMBIENT / ((1 - AMBIENT) * LIGHT_Z)
                extinct = (thick[0] * bumps[0] + thick[1] * bumps[1])
                weight = bumps[0] + bumps[1]
                for k in range(2, terms):
                    extinct = extinct + thick[k] * bumps[k]
                    weight = weight + bumps[k]
                passed = jnp.exp2(extinct * (1.0 - 3.2 * (inv * inv)))
                left = trans * passed
                amount = (trans - left) * (shade / (weight + 1.0))
                total = [total[k] + amount * bumps[k] for k in range(terms)]
                trans = left
                before, current = current, after
            at = pl.multiple_of(row - first_row, 8)
            for c in range(3):
                mixed = total[0] * (colors[c, 0] * ((1 - AMBIENT) * LIGHT_Z))
                for k in range(1, terms):
                    mixed = mixed + total[k] * (colors[c, k] * ((1 - AMBIENT) * LIGHT_Z))
                outs[c, pl.ds(at, 8), :] = mixed
            outs[3, pl.ds(at, 8), :] = trans
        return 0

    lax.fori_loop(0, rows // (8 * ROWS_AT_ONCE), chunk, 0)


def depth_faces(depth_a, depth_b):
    place, count = lax.axis_index("depth"), lax.axis_size("depth")
    even = place % 2 == 0

    def below(row):
        face = jnp.where(even, depth_b[pl.ds(row, 8), :], depth_a[pl.ds(row, 8), :])
        return jnp.where(place > 0, face, 0.0)

    def above(row):
        face = jnp.where(even, depth_a[pl.ds(row, 8), :], depth_b[pl.ds(row, 8), :])
        return jnp.where(place < count - 1, face, 0.0)

    return below, above


def first_kernel(rows_out, start_of, step_len, centers, widths, density, colors, padded, cols, col_a, col_b, row_a, row_b, depth_a, depth_b, full, edges, outs, turned):
    slices, _, lanes = padded.shape
    rows = edges.shape[0]
    left, right = receives(col_a[...], col_b[...], lax.axis_index("ty"), lax.axis_size("ty"))
    turned[...] = jnp.zeros_like(turned)
    for h in range(rows // lanes):
        turned[h, pl.ds(0, slices, 2), :] = right[h] - cols[0, h]
        turned[h, pl.ds(1, slices, 2), :] = cols[1, h] - left[h]
        edges[pl.ds(h * lanes, lanes), :] = turned[h].T
    top, bottom = receives(row_a[...], row_b[...], lax.axis_index("tx"), lax.axis_size("tx"))
    full[:, PAD - 1, :] = top
    full[:, PAD + rows, :] = bottom
    below, above = depth_faces(depth_a, depth_b)
    render(full, edges, below, above, (centers, widths, density, colors), outs, start_of(), rows_out, step_len)


def second_kernel(rows_out, start_of, step_len, centers, widths, density, colors, full, edges, depth_a, depth_b, outs):
    below, above = depth_faces(depth_a, depth_b)
    render(full, edges, below, above, (centers, widths, density, colors), outs, start_of(), rows_out, step_len)


def join_kernel(own, other, image):
    first = lax.axis_index("depth") == 0
    ahead = jnp.where(first, own[3], other[3])
    for c in range(3):
        a, b = own[c], other[c]
        image[c] = jnp.where(first, a, b) + ahead * jnp.where(first, b, a)
    image[3] = 1.0 - own[3] * other[3]


def chain_kernel(parts, image):
    count = parts.shape[0]
    trans = parts[0, 3]
    mix = [parts[0, c] for c in range(3)]
    for d in range(1, count):
        mix = [mix[c] + trans * parts[d, c] for c in range(3)]
        trans = trans * parts[d, 3]
    for c in range(3):
        image[c] = mix[c]
    image[3] = 1.0 - trans


def on_device(volume, centers, widths, density, colors):
    slices, rows, lanes = volume.shape
    depth_count = lax.axis_size("depth")
    part = rows // depth_count
    step_len = 1.0 / (slices * depth_count)
    face = vmem_out(rows, lanes)
    side = (rows // lanes, slices, lanes)
    turned = vmem_out(rows // lanes, lanes, lanes)
    padded, cols, col_a, col_b, row_a, row_b, depth_a, depth_b = pl.pallas_call(
        pack_kernel,
        out_shape=(
            vmem_out(slices, rows + 2 * PAD, lanes),
            vmem_out(2, *side),
            vmem_out(*side),
            vmem_out(*side),
            vmem_out(slices, lanes),
            vmem_out(slices, lanes),
            face,
            face,
        ),
        in_specs=[ANY],
        out_specs=(VMEM,) * 8,
        scratch_shapes=[
            vmem_out(rows, lanes),
            turned,
            pltpu.SemaphoreType.DMA((slices,)),
        ],
        name="pack",
    )(volume)

    depth_rounds = swap_rounds("depth")
    col_rounds = swap_rounds("ty", "tx")
    row_rounds = swap_rounds("tx")

    def send(array, to):
        axes, pairs = to
        return lax.ppermute(array, axes, pairs)

    depth_a = send(depth_a, depth_rounds[0])
    depth_b = send(depth_b, depth_rounds[1]) if depth_count > 2 else depth_a
    col_a = send(col_a, col_rounds[0])
    col_b = send(col_b, col_rounds[1])
    row_a = send(row_a, row_rounds[0])
    row_b = send(row_b, row_rounds[1])
    consts = (centers, widths, density, colors)
    halos = tuple(map(in_vmem, (padded, cols, col_a, col_b, row_a, row_b, depth_a, depth_b)))

    pair = depth_count == 2

    def others_rows():
        return (1 - lax.axis_index("depth")) * part if pair else 0

    def own_rows():
        return lax.axis_index("depth") * part

    sent_rows = part if pair else rows
    full, edges, sent = pl.pallas_call(
        functools.partial(first_kernel, sent_rows, others_rows, step_len),
        out_shape=(
            vmem_out(slices, rows + 2 * PAD, lanes),
            face,
            vmem_out(4, sent_rows, lanes),
        ),
        in_specs=[SMEM] * 4 + [VMEM] * 8,
        out_specs=(VMEM,) * 3,
        scratch_shapes=[turned],
        input_output_aliases={4: 0},
        name="first",
    )(*consts, *halos)
    image = jax.ShapeDtypeStruct((4, part, lanes), jnp.float32)
    if not pair:
        parts = jnp.swapaxes(sent.reshape(4, depth_count, part, lanes), 0, 1)
        parts = lax.all_to_all(parts, "depth", 0, 0)
        return pl.pallas_call(chain_kernel, out_shape=image, name="chain")(parts)
    other = lax.ppermute(sent, "depth", [(0, 1), (1, 0)])
    own = pl.pallas_call(
        functools.partial(second_kernel, part, own_rows, step_len),
        out_shape=vmem_out(4, part, lanes),
        in_specs=[SMEM] * 4 + [VMEM] * 4,
        out_specs=VMEM,
        name="second",
    )(*consts, in_vmem(full), in_vmem(edges), halos[6], halos[7])
    return pl.pallas_call(
        join_kernel,
        out_shape=image,
        in_specs=[VMEM] * 2,
        out_specs=VMEM,
        name="join",
    )(in_vmem(own), in_vmem(other))


def solution(mesh):
    return jax.shard_map(
        on_device,
        mesh=mesh,
        in_specs=(P("depth", "tx", "ty"), P(), P(), P(), P()),
        out_specs=P(None, ("tx", "depth"), "ty"),
        check_vma=False,
    )
```

time: 116 us -> 24.1 us (0.21)
  local copies, waits for them, and re-layouts: 36.5 us -> 0 us
  other arithmetic: 20.3 us -> 0 us
  waiting for transfers between devices: 23 us -> 6.62 us
  between operations: 13.6 us -> 0.03 us
  Pallas kernels: 0 us -> 10.4 us
  blocking collectives: 7.03 us -> 0 us
  starting transfers between devices: 13.5 us -> 6.85 us
  loops' own time: 1.48 us -> 0 us
    squeeze x16 -> x0, local copies, waits for them, and re-layouts: 19.1 us -> none  [advance(): lax.dynamic_index_in_dim(padded, index + 2, 0, keepdims=False)[1:-1, 1:-1]]
    reduce_scatter x1 -> x0, waiting for transfers between devices: 13.5 us -> none  [on_device(): return lax.psum_scatter(terms, 'depth', scatter_dimension=1, tiled=True)]
    slice x21 -> x0, local copies, waits for them, and re-layouts: 10.9 us -> none  [the longest x3 5.62 us: padded_2(): lax.slice_in_dim(cells, cells.shape[dim] - width, cells.shape[dim], axis=...]
    pallas_call x0 -> x4, Pallas kernels: none -> 10.4 us  [the longest x1 3.33 us: on_device(): pl.pallas_call(pack_kernel, out_shape=(vmem_out(slices, rows + 2 * PAD, l...]
    concatenate x3 -> x0, other arithmetic: 7.18 us -> none  [the longest x2 6.35 us: padded_2(): jnp.concatenate([lax.ppermute(tail, axis, [(i, (i + 1) % count) for i in...]
    all_gather x1 -> x0, blocking collectives: 7.03 us -> none  [carried_in(): gathered = lax.all_gather(part, axis)]
    ppermute x6, starting transfers between devices: 13.5 us -> 6.85 us  [the longest x5 6.25 us: send(): return lax.ppermute(array, axes, pairs)]
    reduce_sum x32 -> x0, other arithmetic: 6.54 us -> none  [the longest x16 3.71 us: composite(): jnp.sum(density[:, None, None] * bumps, 0) * (1.0 - 0.8 / (1.0 + grad_sq))]
  transfers between devices with their start and end apart: 7 -> 6, of which waited for: 5 -> 2; matrix products, arithmetic and copies ran while one was open for 6% -> 0% of each run, Pallas kernels for 0% -> 13%
where the time goes in v1:
time: 24.1 us; the launch traced here: 23.9 us
  Pallas kernels  10.4 us (43%)
  starting transfers between devices  6.85 us (28%)
  waiting for transfers between devices  6.62 us (27%)
    ppermute x5, starting transfers between devices, send(): return lax.ppermute(array, axes, pairs)  6.25 us
    ppermute x1, waiting for transfers between devices, on_device(): other = lax.ppermute(sent, 'depth', [(0, 1), (1, 0)])  4.66 us
    pallas_call x1, Pallas kernels, on_device(): pl.pallas_call(pack_kernel, out_shape=(vmem_out(slices, rows + 2 * PAD, l...  3.33 us
    pallas_call x1, Pallas kernels, on_device(): pl.pallas_call(functools.partial(first_kernel, sent_rows, others_rows, st...  3.24 us
    pallas_call x1, Pallas kernels, on_device(): pl.pallas_call(functools.partial(second_kernel, part, own_rows, step_len)...  3.12 us
    ppermute x5, waiting for transfers between devices, send(): return lax.ppermute(array, axes, pairs)  1.96 us
    pallas_call x1, Pallas kernels, on_device(): pl.pallas_call(join_kernel, out_shape=image, in_specs=[VMEM] * 2, out_spe...  0.74 us
    ppermute x1, starting transfers between devices, on_device(): other = lax.ppermute(sent, 'depth', [(0, 1), (1, 0)])  0.6 us
  transfers between devices with their start and end apart: 6, of which 2 were waited for; matrix products, arithmetic and copies ran while one was open for 0% of the time, Pallas kernels for 13%

profile of v1, /device:TPU:0, one launch (start us, length us, event | category | flops | bytes accessed | tf_op | source)
XLA Modules:
  0.0 23.9 jit_solution(13566569094845034530)
XLA Ops:
  0.0 3.3 %pack.1 = (f32[16,272,128]{2,1,0:T(8,128)S(1)}, f32[2,2,16,128]{3,2,1,0:T(8,128)S(1)}, f32[2,16,128]{2,1,0:T(8,128)S(1)}, f32[2,16,128]{2,1,0:T(8,128)S(1)}, f32...) custom-call(f32[16,256,128]{2,1,0:T(8,128)} %volume.1), custom_call_target="tpu_custom_call" | custom-call | tf_op jit(solution)/shard_map/pack/pallas_call | solution.py:216
  3.3 3.0 %collective-permute-start.4 = (f32[256,128]{1,0:T(8,128)S(1)}, f32[256,128]{1,0:T(8,128)S(1)}, u32[]{:S(2)}, u32[]{:S(2)}) collective-permute-start(f32[256,128]{1,0:T(8,128)S(1)} %get-tuple-element.21), channel_id=1, source_target_pairs={{0,16},{16,0},{1,17},{17,1},{2,18},{18,2},{3,19},{19,3},{4,20},{20... | collective-permute-start | bytes 393224 | tf_op jit(solution)/shard_map/ppermute | solution.py:244
  6.4 1.6 %collective-permute-start = (f32[2,16,128]{2,1,0:T(8,128)S(1)}, f32[2,16,128]{2,1,0:T(8,128)S(1)}, u32[]{:S(2)}, u32[]{:S(2)}) collective-permute-start(f32[2,16,128]{2,1,0:T(8,128)S(1)} %get-tuple-element.17), channel_id=1, source_target_pairs={{0,1},{1,0},{2,3},{3,2},{4,5},{5,4},{6,7},{7,6},{8,9},{9,8},{10,11... | collective-permute-start | bytes 49160 | tf_op jit(solution)/shard_map/ppermute | solution.py:244
  8.0 0.0 collective-permute-start.1
  8.0 0.5 %collective-permute-start.2 = (f32[16,128]{1,0:T(8,128)S(1)}, f32[16,128]{1,0:T(8,128)S(1)}, u32[]{:S(2)}, u32[]{:S(2)}) collective-permute-start(f32[16,128]{1,0:T(8,128)S(1)} %get-tuple-element.19), channel_id=1, source_target_pairs={{0,4},{4,0},{8,12},{12,8},{1,5},{5,1},{9,13},{13,9},{2,6},{6,2},{1... | collective-permute-start | bytes 24584 | tf_op jit(solution)/shard_map/ppermute | solution.py:244
  8.5 1.1 %collective-permute-start.3 = (f32[16,128]{1,0:T(8,128)S(1)}, f32[16,128]{1,0:T(8,128)S(1)}, u32[]{:S(2)}, u32[]{:S(2)}) collective-permute-start(f32[16,128]{1,0:T(8,128)S(1)} %get-tuple-element.20), channel_id=1, source_target_pairs={{0,12},{4,8},{8,4},{12,0},{1,13},{5,9},{9,5},{13,1},{2,14},{6,10},... | collective-permute-start | bytes 24584 | tf_op jit(solution)/shard_map/ppermute | solution.py:244
  9.6 0.0 collective-permute-done.2.row_a
  9.6 1.9 %collective-permute-done.3.row_b = f32[16,128]{1,0:T(8,128)S(1)} collective-permute-done((f32[16,128]{1,0:T(8,128)S(1)}, f32[16,128]{1,0:T(8,128)S(1)}, u32[]{:S(2)}, u32[]{:S(2)}) %collective-permute-start.3) | collective-permute-done | bytes 8224 | tf_op jit(solution)/shard_map/ppermute | solution.py:244
  11.5 0.0 collective-permute-done.col_a
  11.5 0.0 collective-permute-done.1.col_b
  11.5 0.0 collective-permute-done.4.depth_a.depth_b
  11.6 3.2 %first.1 = (f32[16,272,128]{2,1,0:T(8,128)S(1)}, f32[256,128]{1,0:T(8,128)S(1)}, f32[4,128,128]{2,1,0:T(8,128)S(1)}) custom-call(f32[4]{0:T(128)} %centers.3, f32[4]{0:T(128)} %widths.3, f32[4]{0:T(128)} %density.3, f32[3,4]{1,0:T(4,128)} %colors.3, f32[16,272,128]{2,1,0:T(8,128)S(1)} %get-tuple-element.15.padded, ...), custom_call_target="tpu_custom_call", output_to_operand_aliasing={{0}: (4, {})} | custom-call | tf_op jit(solution)/shard_map/first/pallas_call | solution.py:264
  14.8 0.6 %collective-permute-start.5 = (f32[4,128,128]{2,1,0:T(8,128)S(1)}, f32[4,128,128]{2,1,0:T(8,128)S(1)}, u32[]{:S(2)}, u32[]{:S(2)}) collective-permute-start(f32[4,128,128]{2,1,0:T(8,128)S(1)} %get-tuple-element.24), channel_id=1, source_target_pairs={{0,16},{16,0},{1,17},{17,1},{2,18},{18,2},{3,19},{19,3},{4,20},{20... | collective-permute-start | bytes 786440 | tf_op jit(solution)/shard_map/ppermute | solution.py:282
  15.4 3.1 %second.1.own = f32[4,128,128]{2,1,0:T(8,128)S(1)} custom-call(f32[4]{0:T(128)} %centers.3, f32[4]{0:T(128)} %widths.3, f32[4]{0:T(128)} %density.3, f32[3,4]{1,0:T(4,128)} %colors.3, f32[16,272,128]{2,1,0:T(8,128)S(1)} %get-tuple-element.22.full, f32[256,128]{1,0:T(8,128)S(1)} %get-tuple-element.23.edges, ...), custom_call_target="tpu_custom_call" | custom-call | tf_op jit(solution)/shard_map/second/pallas_call | solution.py:283
  18.5 4.7 %collective-permute-done.5.other = f32[4,128,128]{2,1,0:T(8,128)S(1)} collective-permute-done((f32[4,128,128]{2,1,0:T(8,128)S(1)}, f32[4,128,128]{2,1,0:T(8,128)S(1)}, u32[]{:S(2)}, u32[]{:S(2)}) %collective-permute-start.5) | collective-permute-done | bytes 262176 | tf_op jit(solution)/shard_map/ppermute | solution.py:282
  23.2 0.7 %join.1 = f32[4,128,128]{2,1,0:T(8,128)} custom-call(f32[4,128,128]{2,1,0:T(8,128)S(1)} %second.1.own, f32[4,128,128]{2,1,0:T(8,128)S(1)} %collective-permute-done.5.other), custom_call_target="tpu_custom_call" | custom-call | tf_op jit(solution)/shard_map/join/pallas_call | solution.py:290
Async XLA Ops:
  3.3 8.2 %collective-permute-start.4 = (f32[256,128]{1,0:T(8,128)S(1)}, f32[256,128]{1,0:T(8,128)S(1)}, u32[]{:S(2)}, u32[]{:S(2)}) collective-permute-start(f32[256,128]{1,0:T(8,128)S(1)} %get-tuple-element.21), channel_id=1, source_target_pairs={{0,16},{16,0},{1,17},{17,1},{2,18},{18,2},{3,19},{19,3},{4,20},{20... | collective-permute-start | bytes 393224 | tf_op jit(solution)/shard_map/ppermute | solution.py:244
  6.4 5.2 %collective-permute-start = (f32[2,16,128]{2,1,0:T(8,128)S(1)}, f32[2,16,128]{2,1,0:T(8,128)S(1)}, u32[]{:S(2)}, u32[]{:S(2)}) collective-permute-start(f32[2,16,128]{2,1,0:T(8,128)S(1)} %get-tuple-element.17), channel_id=1, source_target_pairs={{0,1},{1,0},{2,3},{3,2},{4,5},{5,4},{6,7},{7,6},{8,9},{9,8},{10,11... | collective-permute-start | bytes 49160 | tf_op jit(solution)/shard_map/ppermute | solution.py:244
  8.0 3.6 %collective-permute-start.1 = (f32[2,16,128]{2,1,0:T(8,128)S(1)}, f32[2,16,128]{2,1,0:T(8,128)S(1)}, u32[]{:S(2)}, u32[]{:S(2)}) collective-permute-start(f32[2,16,128]{2,1,0:T(8,128)S(1)} %get-tuple-element.18), channel_id=1, source_target_pairs={{0,4},{1,2},{2,1},{3,7},{4,0},{5,6},{6,5},{7,3},{8,12},{9,10},{10,... | collective-permute-start | bytes 49160 | tf_op jit(solution)/shard_map/ppermute | solution.py:244
  8.0 1.6 %collective-permute-start.2 = (f32[16,128]{1,0:T(8,128)S(1)}, f32[16,128]{1,0:T(8,128)S(1)}, u32[]{:S(2)}, u32[]{:S(2)}) collective-permute-start(f32[16,128]{1,0:T(8,128)S(1)} %get-tuple-element.19), channel_id=1, source_target_pairs={{0,4},{4,0},{8,12},{12,8},{1,5},{5,1},{9,13},{13,9},{2,6},{6,2},{1... | collective-permute-start | bytes 24584 | tf_op jit(solution)/shard_map/ppermute | solution.py:244
  8.5 3.1 %collective-permute-start.3 = (f32[16,128]{1,0:T(8,128)S(1)}, f32[16,128]{1,0:T(8,128)S(1)}, u32[]{:S(2)}, u32[]{:S(2)}) collective-permute-start(f32[16,128]{1,0:T(8,128)S(1)} %get-tuple-element.20), channel_id=1, source_target_pairs={{0,12},{4,8},{8,4},{12,0},{1,13},{5,9},{9,5},{13,1},{2,14},{6,10},... | collective-permute-start | bytes 24584 | tf_op jit(solution)/shard_map/ppermute | solution.py:244
  14.8 8.4 %collective-permute-start.5 = (f32[4,128,128]{2,1,0:T(8,128)S(1)}, f32[4,128,128]{2,1,0:T(8,128)S(1)}, u32[]{:S(2)}, u32[]{:S(2)}) collective-permute-start(f32[4,128,128]{2,1,0:T(8,128)S(1)} %get-tuple-element.24), channel_id=1, source_target_pairs={{0,16},{16,0},{1,17},{17,1},{2,18},{18,2},{3,19},{19,3},{4,20},{20... | collective-permute-start | bytes 786440 | tf_op jit(solution)/shard_map/ppermute | solution.py:282

commit v2 on v1

v2 whole, which is shorter than its diff:
```python
import functools
import math

import jax
import jax.numpy as jnp
from jax import lax
from jax.experimental import pallas as pl
from jax.experimental.pallas import tpu as pltpu
from jax.sharding import PartitionSpec as P

LIGHT_X = 0.36
LIGHT_Y = 0.48
LIGHT_Z = 0.8
AMBIENT = 0.2
PAD = 8
ROWS_AT_ONCE = 4
LOADS = 4

ANY = pl.BlockSpec(memory_space=pl.ANY)
VMEM = pl.BlockSpec(memory_space=pltpu.VMEM)
ROOM = pltpu.CompilerParams(vmem_limit_bytes=8 << 20)
SMEM = pl.BlockSpec(memory_space=pltpu.SMEM)


def in_vmem(array):
    return pltpu.with_memory_space_constraint(array, pltpu.VMEM)


def in_hbm(array):
    return pltpu.with_memory_space_constraint(array, pltpu.HBM)


def vmem_out(*shape):
    return pltpu.VMEM(shape, jnp.float32)


def sends(low, high, even):
    return jnp.where(even, high, low), jnp.where(even, low, high)


def receives(first, second, place, count):
    even = place % 2 == 0
    low = jnp.where(even, second, first)
    high = jnp.where(even, first, second)
    return jnp.where(place > 0, low, 0.0), jnp.where(place < count - 1, high, 0.0)


def swap_rounds(axis, beside=None):
    count = lax.axis_size(axis)
    first = [(i, i ^ 1) for i in range(count)]
    inner = {i: (i + 1 if i % 2 else i - 1) for i in range(1, count - 1)}
    if beside is None or lax.axis_size(beside) % 2:
        second = [(i, inner.get(i, count - 1 - i)) for i in range(count)]
        return (axis, first), (axis, second)
    second = []
    for b in range(lax.axis_size(beside)):
        for i in range(count):
            to = (b, inner[i]) if i in inner else (b ^ 1, i)
            second.append((b * count + i, to[0] * count + to[1]))
    return (axis, first), ((beside, axis), second)


def pack_kernel(volume, padded, cols, col_a, col_b, row_a, row_b, *rest):
    *depth, packed, turned, sems = rest
    slices, rows, lanes = volume.shape

    group = slices // sems.shape[0]

    def copy(g):
        some = pl.ds(g * group, group)
        return pltpu.make_async_copy(
            volume.at[some], padded.at[some, pl.ds(PAD, rows), :], sems.at[g]
        )

    for g in range(sems.shape[0]):
        copy(g).start()
    lane = lax.broadcasted_iota(jnp.int32, (rows, lanes), 1)
    packed[...] = jnp.zeros_like(packed)
    for s in range(slices):
        if s % group == 0:
            copy(s // group).wait()
        moved = pltpu.roll(padded[s, pl.ds(PAD, rows), :], 2 * s + 1, 1)
        packed[...] = jnp.where(lane // 2 == s, moved, packed[...])
    even_y = lax.axis_index("ty") % 2 == 0
    for h in range(rows // lanes):
        turned[h] = packed[pl.ds(h * lanes, lanes), :].T
        last = turned[h, pl.ds(0, slices, 2), :]
        first = turned[h, pl.ds(1, slices, 2), :]
        cols[0, h] = first
        cols[1, h] = last
        col_a[h], col_b[h] = sends(first, last, even_y)
    even_x = lax.axis_index("tx") % 2 == 0
    row_a[...], row_b[...] = sends(padded[:, PAD, :], padded[:, PAD + rows - 1, :], even_x)
    even_z = lax.axis_index("depth") % 2 == 0
    low = padded[0, pl.ds(PAD, rows), :]
    high = padded[slices - 1, pl.ds(PAD, rows), :]
    faces = sends(low, high, even_z)
    for ref, face in zip(depth, faces):
        ref[...] = face


def constants(consts, tile, step_len):
    centers, widths, density, _ = consts
    log2e = math.log2(math.e)

    def splat(x):
        return jnp.full(tile, x, jnp.float32)

    terms = range(centers.shape[0])
    beta = [splat(-log2e) / (splat(widths[k]) * splat(widths[k])) for k in terms]
    thick = [splat(density[k]) * (-log2e * step_len) for k in terms]
    return [splat(centers[k]) for k in terms], beta, thick


def transfer(current, centre, beta, thick):
    bumps = []
    for k in range(len(beta)):
        off = current - centre[k]
        bumps.append(jnp.exp2(off * beta[k] * off))
    extinct, weight = thick[0] * bumps[0], bumps[0] + 1.0
    for k in range(1, len(beta)):
        extinct = extinct + thick[k] * bumps[k]
        weight = weight + bumps[k]
    return bumps, extinct, weight


def prepare(padded, consts, pre, first_row, step_len):
    count, slices, rows, lanes = pre.shape
    tile = (8, lanes)
    values = constants(consts, tile, step_len)

    def chunk(index, _):
        for j in range(ROWS_AT_ONCE):
            at = pl.multiple_of((index * ROWS_AT_ONCE + j) * 8, 8)
            row = pl.multiple_of(first_row + at, 8)
            for s in range(slices):
                bumps, extinct, weight = transfer(padded[s, pl.ds(row + PAD, 8), :], *values)
                share = 1.0 / weight
                for k in range(count - 1):
                    pre[k, s, pl.ds(at, 8), :] = bumps[k] * share
                pre[count - 1, s, pl.ds(at, 8), :] = extinct
        return 0

    lax.fori_loop(0, rows // (8 * ROWS_AT_ONCE), chunk, 0)


def render(padded, edges, below, above, consts, outs, first_row, step_len, pre=None, pre_row=0):
    colors = consts[3]
    slices, _, lanes = padded.shape
    rows = outs.shape[1]
    terms = colors.shape[1]
    tile = (8, lanes)
    values = constants(consts, tile, step_len) if pre is None else None
    lane = lax.broadcasted_iota(jnp.int32, tile, 1)
    edge = (lane == 0) | (lane == lanes - 1)
    zero, one = jnp.zeros(tile, jnp.float32), jnp.ones(tile, jnp.float32)

    def chunk(index, _):
        for j in range(ROWS_AT_ONCE):
            at = pl.multiple_of((index * ROWS_AT_ONCE + j) * 8, 8)
            row = pl.multiple_of(first_row + at, 8)
            pre_at = pl.multiple_of(pre_row + at, 8)
            edge_rows = edges[pl.ds(row, 8), :]
            total, trans = [zero] * terms, one
            before = below(row)
            current = padded[0, pl.ds(row + PAD, 8), :]
            for s in range(slices):
                after = padded[s + 1, pl.ds(row + PAD, 8), :] if s + 1 < slices else above(row)
                dx = padded[s, pl.ds(row + PAD + 1, 8), :] - padded[s, pl.ds(row + PAD - 1, 8), :]
                dy = pltpu.roll(current, lanes - 1, 1) - pltpu.roll(current, 1, 1)
                dy = dy + jnp.where(edge, pltpu.roll(edge_rows, lanes - (2 * s + 1), 1), 0.0)
                dz = after - before
                inv = lax.rsqrt((dx * dx + dy * dy) + (dz * dz + 4.0))
                lit = jnp.abs(dx * (LIGHT_X / LIGHT_Z) + dy * (LIGHT_Y / LIGHT_Z) + dz)
                shade = lit * inv + AMBIENT / ((1 - AMBIENT) * LIGHT_Z)
                if pre is None:
                    bumps, extinct, weight = transfer(current, *values)
                    shade = shade / weight
                else:
                    bumps = [pre[k, s, pl.ds(pre_at, 8), :] for k in range(terms)]
                    extinct = pre[terms, s, pl.ds(pre_at, 8), :]
                passed = jnp.exp2(extinct * (1.0 - 3.2 * (inv * inv)))
                left = trans * passed
                amount = (trans - left) * shade
                total = [total[k] + amount * bumps[k] for k in range(terms)]
                trans = left
                before, current = current, after
            for c in range(3):
                mixed = total[0] * (colors[c, 0] * ((1 - AMBIENT) * LIGHT_Z))
                for k in range(1, terms):
                    mixed = mixed + total[k] * (colors[c, k] * ((1 - AMBIENT) * LIGHT_Z))
                outs[c, pl.ds(at, 8), :] = mixed
            outs[3, pl.ds(at, 8), :] = trans
        return 0

    lax.fori_loop(0, rows // (8 * ROWS_AT_ONCE), chunk, 0)


def depth_faces(depth_a, depth_b):
    place, count = lax.axis_index("depth"), lax.axis_size("depth")
    even = place % 2 == 0

    def below(row):
        face = jnp.where(even, depth_b[pl.ds(row, 8), :], depth_a[pl.ds(row, 8), :])
        return jnp.where(place > 0, face, 0.0)

    def above(row):
        face = jnp.where(even, depth_a[pl.ds(row, 8), :], depth_b[pl.ds(row, 8), :])
        return jnp.where(place < count - 1, face, 0.0)

    return below, above


def turn_edges(cols, col_a, col_b, edges, turned):
    _, chunks, slices, lanes = cols.shape
    left, right = receives(col_a[...], col_b[...], lax.axis_index("ty"), lax.axis_size("ty"))
    turned[...] = jnp.zeros_like(turned)
    for h in range(chunks):
        turned[h, pl.ds(0, slices, 2), :] = right[h] - cols[0, h]
        turned[h, pl.ds(1, slices, 2), :] = cols[1, h] - left[h]
        edges[pl.ds(h * lanes, lanes), :] = turned[h].T


def fill_rows(row_a, row_b, full):
    top, bottom = receives(row_a[...], row_b[...], lax.axis_index("tx"), lax.axis_size("tx"))
    full[:, PAD - 1, :] = top
    full[:, full.shape[1] - PAD, :] = bottom


def partner_rows(rows, inner):
    ahead = lax.axis_index("depth") == 0
    quarter = rows // 4
    at = jnp.where(ahead == inner, 0, quarter)
    return pl.multiple_of(jnp.where(ahead, 2 * quarter, 0) + at, 8), pl.multiple_of(at, 8)


def before_kernel(step_len, centers, widths, density, colors, padded, pre):
    rows = 2 * pre.shape[2]
    start = pl.multiple_of((1 - lax.axis_index("depth")) * (rows // 2), 8)
    prepare(padded, (centers, widths, density, colors), pre, start, step_len)


def inner_kernel(step_len, centers, widths, density, colors, padded, pre, cols, col_a, col_b, depth_a, edges, outs, turned):
    turn_edges(cols, col_a, col_b, edges, turned)
    below, above = depth_faces(depth_a, depth_a)
    row, pre_row = partner_rows(edges.shape[0], True)
    render(padded, edges, below, above, (centers, widths, density, colors), outs, row, step_len, pre, pre_row)


def outer_kernel(step_len, centers, widths, density, colors, padded, pre, edges, row_a, row_b, depth_a, full, outs):
    fill_rows(row_a, row_b, full)
    below, above = depth_faces(depth_a, depth_a)
    row, pre_row = partner_rows(edges.shape[0], False)
    render(full, edges, below, above, (centers, widths, density, colors), outs, row, step_len, pre, pre_row)


def own_kernel(step_len, centers, widths, density, colors, full, edges, depth_a, outs):
    below, above = depth_faces(depth_a, depth_a)
    row = pl.multiple_of(lax.axis_index("depth") * outs.shape[1], 8)
    render(full, edges, below, above, (centers, widths, density, colors), outs, row, step_len)


def whole_kernel(step_len, centers, widths, density, colors, padded, cols, col_a, col_b, row_a, row_b, depth_a, depth_b, full, outs, edges, turned):
    turn_edges(cols, col_a, col_b, edges, turned)
    fill_rows(row_a, row_b, full)
    below, above = depth_faces(depth_a, depth_b)
    render(full, edges, below, above, (centers, widths, density, colors), outs, 0, step_len)


def join_kernel(own, inner, outer, image):
    ahead = lax.axis_index("depth") == 0
    rows = inner.shape[1]
    for part, at in ((inner, jnp.where(ahead, rows, 0)), (outer, jnp.where(ahead, 0, rows))):
        some = pl.ds(pl.multiple_of(at, 8), rows)
        trans = jnp.where(ahead, own[3, some], part[3])
        for c in range(3):
            a, b = own[c, some], part[c]
            image[c, some] = jnp.where(ahead, a, b) + trans * jnp.where(ahead, b, a)
        image[3, some] = 1.0 - own[3, some] * part[3]


def chain_kernel(parts, image):
    count = parts.shape[0]
    trans = parts[0, 3]
    mix = [parts[0, c] for c in range(3)]
    for d in range(1, count):
        mix = [mix[c] + trans * parts[d, c] for c in range(3)]
        trans = trans * parts[d, 3]
    for c in range(3):
        image[c] = mix[c]
    image[3] = 1.0 - trans


def swap(array, to):
    axes, pairs = to
    return in_vmem(lax.ppermute(array, axes, pairs))


def on_device(volume, centers, widths, density, colors):
    slices, rows, lanes = volume.shape
    depth_count = lax.axis_size("depth")
    pair = depth_count == 2
    part = rows // depth_count
    step_len = 1.0 / (slices * depth_count)
    consts = tuple(map(in_hbm, (centers, widths, density, colors)))
    block = vmem_out(slices, rows + 2 * PAD, lanes)
    face = vmem_out(rows, lanes)
    side = (rows // lanes, slices, lanes)
    turned = vmem_out(rows // lanes, lanes, lanes)
    image = jax.ShapeDtypeStruct((4, part, lanes), jnp.float32)
    out_shape = (block, vmem_out(2, *side)) + (vmem_out(*side),) * 2 + (vmem_out(slices, lanes),) * 2 + (face,) * (1 if pair else 2)
    padded, cols, col_a, col_b, row_a, row_b, *depth = pl.pallas_call(
        pack_kernel,
        out_shape=out_shape,
        in_specs=[ANY],
        out_specs=(VMEM,) * len(out_shape),
        scratch_shapes=[face, turned, pltpu.SemaphoreType.DMA((math.gcd(slices, LOADS),))],
        compiler_params=ROOM,
        name="pack",
    )(in_hbm(volume))
    padded, cols = in_vmem(padded), in_vmem(cols)

    depth = [swap(array, to) for array, to in zip(depth, swap_rounds("depth"))]
    col_a, col_b = (swap(array, to) for array, to in zip((col_a, col_b), swap_rounds("ty", "tx")))
    row_rounds = swap_rounds("tx")
    row_a = swap(row_a, row_rounds[0])
    row_b = swap(row_b, row_rounds[1])

    def call(kernel, out_shape, args, scratch=(), aliases={}):
        return pl.pallas_call(
            functools.partial(kernel, step_len),
            out_shape=out_shape,
            in_specs=[SMEM] * 4 + [VMEM] * len(args),
            out_specs=jax.tree.map(lambda _: VMEM, out_shape),
            scratch_shapes=scratch,
            input_output_aliases=aliases,
            compiler_params=ROOM,
        )(*consts, *args)

    if not pair:
        _, sent = call(
            whole_kernel,
            (block, vmem_out(4, rows, lanes)),
            (padded, cols, col_a, col_b, row_a, row_b, *depth),
            [face, turned],
            {4: 0},
        )
        parts = jnp.swapaxes(sent.reshape(4, depth_count, part, lanes), 0, 1)
        parts = lax.all_to_all(parts, "depth", 0, 0)
        return pl.pallas_call(chain_kernel, out_shape=image, compiler_params=ROOM, name="chain")(parts)

    both = ("depth", [(0, 1), (1, 0)])
    pre = in_vmem(call(before_kernel, vmem_out(colors.shape[1] + 1, slices, part, lanes), (padded,)))
    edges, inner = call(
        inner_kernel, (face, vmem_out(4, part // 2, lanes)), (padded, pre, cols, col_a, col_b, *depth), [turned]
    )
    edges = in_vmem(edges)
    other_inner = swap(inner, both)
    full, outer = call(
        outer_kernel, (block, vmem_out(4, part // 2, lanes)), (padded, pre, edges, row_a, row_b, *depth), aliases={4: 0}
    )
    other_outer = swap(outer, both)
    own = call(own_kernel, vmem_out(4, part, lanes), (in_vmem(full), edges, *depth))
    return pl.pallas_call(
        join_kernel,
        out_shape=image,
        in_specs=[VMEM] * 3,
        out_specs=VMEM,
        compiler_params=ROOM,
        name="join",
    )(in_vmem(own), other_inner, other_outer)


def solution(mesh):
    return jax.shard_map(
        on_device,
        mesh=mesh,
        in_specs=(P("depth", "tx", "ty"), P(), P(), P(), P()),
        out_specs=P(None, ("tx", "depth"), "ty"),
        check_vma=False,
    )
```

time: 24.1 us -> 23.1 us (0.959)
  waiting for transfers between devices: 6.62 us -> 3.59 us
  starting transfers between devices: 6.85 us -> 8.34 us
  Pallas kernels: 10.4 us -> 10.8 us
    ppermute x6 -> x7, waiting for transfers between devices: 6.62 us -> 3.59 us  [swap(): return in_vmem(lax.ppermute(array, axes, pairs))]
    ppermute x6 -> x7, starting transfers between devices: 6.85 us -> 8.34 us  [swap(): return in_vmem(lax.ppermute(array, axes, pairs))]
    pallas_call x4 -> x6, Pallas kernels: 10.4 us -> 10.8 us  [the longest x4 8.12 us: call(): pl.pallas_call(functools.partial(kernel, step_len), out_shape=out_shape,...]
  transfers between devices with their start and end apart: 6 -> 7, of which waited for: 2 -> 2; matrix products, arithmetic and copies ran while one was open for 0% -> 0% of each run, Pallas kernels for 13% -> 29%
where the time goes in v2:
time: 23.1 us; the launch traced here: 22.8 us
  Pallas kernels  10.8 us (47%)
  starting transfers between devices  8.34 us (36%)
  waiting for transfers between devices  3.59 us (16%)
    ppermute x7, starting transfers between devices, swap(): return in_vmem(lax.ppermute(array, axes, pairs))  8.34 us
    pallas_call x4, Pallas kernels, call(): pl.pallas_call(functools.partial(kernel, step_len), out_shape=out_shape,...  8.12 us
    ppermute x7, waiting for transfers between devices, swap(): return in_vmem(lax.ppermute(array, axes, pairs))  3.59 us
    pallas_call x1, Pallas kernels, on_device(): pl.pallas_call(pack_kernel, out_shape=out_shape, in_specs=[ANY], out_spec...  1.96 us
    pallas_call x1, Pallas kernels, on_device(): pl.pallas_call(join_kernel, out_shape=image, in_specs=[VMEM] * 3, out_spe...  0.74 us
  transfers between devices with their start and end apart: 7, of which 2 were waited for; matrix products, arithmetic and copies ran while one was open for 0% of the time, Pallas kernels for 29%

profile of v2, /device:TPU:0, one launch (start us, length us, event | category | flops | bytes accessed | tf_op | source)
XLA Modules:
  0.0 22.8 jit_solution(5346857122678591273)
XLA Ops:
  0.0 2.0 %pack.1 = (f32[16,272,128]{2,1,0:T(8,128)S(1)}, f32[2,2,16,128]{3,2,1,0:T(8,128)S(1)}, f32[2,16,128]{2,1,0:T(8,128)S(1)}, f32[2,16,128]{2,1,0:T(8,128)S(1)}, f32...) custom-call(f32[16,256,128]{2,1,0:T(8,128)} %volume.1), custom_call_target="tpu_custom_call" | custom-call | tf_op jit(solution)/shard_map/pack/pallas_call | solution.py:312
  2.0 3.0 %collective-permute-start.2 = (f32[256,128]{1,0:T(8,128)S(1)}, f32[256,128]{1,0:T(8,128)S(1)}, u32[]{:S(2)}, u32[]{:S(2)}) collective-permute-start(f32[256,128]{1,0:T(8,128)S(1)} %get-tuple-element.20), channel_id=1, source_target_pairs={{0,16},{16,0},{1,17},{17,1},{2,18},{18,2},{3,19},{19,3},{4,20},{20... | collective-permute-start | bytes 393224 | tf_op jit(solution)/shard_map/ppermute | solution.py:296
  5.0 1.6 %collective-permute-start = (f32[2,16,128]{2,1,0:T(8,128)S(1)}, f32[2,16,128]{2,1,0:T(8,128)S(1)}, u32[]{:S(2)}, u32[]{:S(2)}) collective-permute-start(f32[2,16,128]{2,1,0:T(8,128)S(1)} %get-tuple-element.18), channel_id=1, source_target_pairs={{0,1},{1,0},{2,3},{3,2},{4,5},{5,4},{6,7},{7,6},{8,9},{9,8},{10,11... | collective-permute-start | bytes 49160 | tf_op jit(solution)/shard_map/ppermute | solution.py:296
  6.6 0.0 collective-permute-start.1
  6.6 0.5 %collective-permute-start.3 = (f32[16,128]{1,0:T(8,128)S(1)}, f32[16,128]{1,0:T(8,128)S(1)}, u32[]{:S(2)}, u32[]{:S(2)}) collective-permute-start(f32[16,128]{1,0:T(8,128)S(1)} %get-tuple-element.22), channel_id=1, source_target_pairs={{0,4},{4,0},{8,12},{12,8},{1,5},{5,1},{9,13},{13,9},{2,6},{6,2},{1... | collective-permute-start | bytes 24584 | tf_op jit(solution)/shard_map/ppermute | solution.py:296
  7.1 1.1 %collective-permute-start.4 = (f32[16,128]{1,0:T(8,128)S(1)}, f32[16,128]{1,0:T(8,128)S(1)}, u32[]{:S(2)}, u32[]{:S(2)}) collective-permute-start(f32[16,128]{1,0:T(8,128)S(1)} %get-tuple-element.23), channel_id=1, source_target_pairs={{0,12},{4,8},{8,4},{12,0},{1,13},{5,9},{9,5},{13,1},{2,14},{6,10},... | collective-permute-start | bytes 24584 | tf_op jit(solution)/shard_map/ppermute | solution.py:296
  8.2 1.9 %shard_map.55.pre = f32[5,16,128,128]{3,2,1,0:T(8,128)S(1)} custom-call(f32[4]{0:T(128)} %centers.7, f32[4]{0:T(128)} %widths.7, f32[4]{0:T(128)} %density.7, f32[3,4]{1,0:T(4,128)} %colors.7, f32[16,272,128]{2,1,0:T(8,128)S(1)} %get-tuple-element.16.padded), custom_call_target="tpu_custom_call" | custom-call | tf_op jit(solution)/shard_map/pallas_call | solution.py:330
  10.1 0.0 collective-permute-done.col_a
  10.1 0.0 collective-permute-done.1.col_b
  10.1 0.0 collective-permute-done.2.depth_a
  10.1 1.6 %shard_map.56 = (f32[256,128]{1,0:T(8,128)S(1)}, f32[4,64,128]{2,1,0:T(8,128)S(1)}) custom-call(f32[4]{0:T(128)} %centers.7, f32[4]{0:T(128)} %widths.7, f32[4]{0:T(128)} %density.7, f32[3,4]{1,0:T(4,128)} %colors.7, f32[16,272,128]{2,1,0:T(8,128)S(1)} %get-tuple-element.16.padded, f32[5,16,128,128]{3,2,1,0:T(8,128)S(1)} %shard_map.55.pre, ...), custom_call_target="tpu_custom_call" | custom-call | tf_op jit(solution)/shard_map/pallas_call | solution.py:330
  11.7 0.0 collective-permute-done.3.row_a
  11.8 0.0 collective-permute-done.4.row_b
  11.8 1.5 %shard_map.57 = (f32[16,272,128]{2,1,0:T(8,128)S(1)}, f32[4,64,128]{2,1,0:T(8,128)S(1)}) custom-call(f32[4]{0:T(128)} %centers.7, f32[4]{0:T(128)} %widths.7, f32[4]{0:T(128)} %density.7, f32[3,4]{1,0:T(4,128)} %colors.7, f32[16,272,128]{2,1,0:T(8,128)S(1)} %get-tuple-element.16.padded, ...), custom_call_target="tpu_custom_call", output_to_operand_aliasing={{0}: (4, {})} | custom-call | tf_op jit(solution)/shard_map/pallas_call | solution.py:330
  13.3 0.6 %collective-permute-start.6 = (f32[4,64,128]{2,1,0:T(8,128)S(1)}, f32[4,64,128]{2,1,0:T(8,128)S(1)}, u32[]{:S(2)}, u32[]{:S(2)}) collective-permute-start(f32[4,64,128]{2,1,0:T(8,128)S(1)} %get-tuple-element.26), channel_id=1, source_target_pairs={{0,16},{16,0},{1,17},{17,1},{2,18},{18,2},{3,19},{19,3},{4,20},{20... | collective-permute-start | bytes 393224 | tf_op jit(solution)/shard_map/ppermute | solution.py:296
  13.9 1.5 %collective-permute-start.5 = (f32[4,64,128]{2,1,0:T(8,128)S(1)}, f32[4,64,128]{2,1,0:T(8,128)S(1)}, u32[]{:S(2)}, u32[]{:S(2)}) collective-permute-start(f32[4,64,128]{2,1,0:T(8,128)S(1)} %get-tuple-element.25), channel_id=1, source_target_pairs={{0,16},{16,0},{1,17},{17,1},{2,18},{18,2},{3,19},{19,3},{4,20},{20... | collective-permute-start | bytes 393224 | tf_op jit(solution)/shard_map/ppermute | solution.py:296
  15.4 3.1 %shard_map.58.own = f32[4,128,128]{2,1,0:T(8,128)S(1)} custom-call(f32[4]{0:T(128)} %centers.7, f32[4]{0:T(128)} %widths.7, f32[4]{0:T(128)} %density.7, f32[3,4]{1,0:T(4,128)} %colors.7, f32[16,272,128]{2,1,0:T(8,128)S(1)} %get-tuple-element.24.full, f32[256,128]{1,0:T(8,128)S(1)} %get-tuple-element.21.edges, f32[256,128]{1,0:T(8,128)S(1)} %collective-permute-done.2.depth_a), custom_call_target="tpu_custom_call" | custom-call | tf_op jit(solution)/shard_map/pallas_call | solution.py:330
  18.5 1.2 %collective-permute-done.6.outer = f32[4,64,128]{2,1,0:T(8,128)S(1)} collective-permute-done((f32[4,64,128]{2,1,0:T(8,128)S(1)}, f32[4,64,128]{2,1,0:T(8,128)S(1)}, u32[]{:S(2)}, u32[]{:S(2)}) %collective-permute-start.6) | collective-permute-done | bytes 131104 | tf_op jit(solution)/shard_map/ppermute | solution.py:296
  19.7 2.3 %collective-permute-done.5.inner = f32[4,64,128]{2,1,0:T(8,128)S(1)} collective-permute-done((f32[4,64,128]{2,1,0:T(8,128)S(1)}, f32[4,64,128]{2,1,0:T(8,128)S(1)}, u32[]{:S(2)}, u32[]{:S(2)}) %collective-permute-start.5) | collective-permute-done | bytes 131104 | tf_op jit(solution)/shard_map/ppermute | solution.py:296
  22.1 0.7 %join.1 = f32[4,128,128]{2,1,0:T(8,128)} custom-call(f32[4,128,128]{2,1,0:T(8,128)S(1)} %shard_map.58.own, f32[4,64,128]{2,1,0:T(8,128)S(1)} %collective-permute-done.5.inner, f32[4,64,128]{2,1,0:T(8,128)S(1)} %collective-permute-done.6.outer), custom_call_target="tpu_custom_call" | custom-call | tf_op jit(solution)/shard_map/join/pallas_call | solution.py:364
Async XLA Ops:
  2.0 8.2 %collective-permute-start.2 = (f32[256,128]{1,0:T(8,128)S(1)}, f32[256,128]{1,0:T(8,128)S(1)}, u32[]{:S(2)}, u32[]{:S(2)}) collective-permute-start(f32[256,128]{1,0:T(8,128)S(1)} %get-tuple-element.20), channel_id=1, source_target_pairs={{0,16},{16,0},{1,17},{17,1},{2,18},{18,2},{3,19},{19,3},{4,20},{20... | collective-permute-start | bytes 393224 | tf_op jit(solution)/shard_map/ppermute | solution.py:296
  5.0 5.1 %collective-permute-start = (f32[2,16,128]{2,1,0:T(8,128)S(1)}, f32[2,16,128]{2,1,0:T(8,128)S(1)}, u32[]{:S(2)}, u32[]{:S(2)}) collective-permute-start(f32[2,16,128]{2,1,0:T(8,128)S(1)} %get-tuple-element.18), channel_id=1, source_target_pairs={{0,1},{1,0},{2,3},{3,2},{4,5},{5,4},{6,7},{7,6},{8,9},{9,8},{10,11... | collective-permute-start | bytes 49160 | tf_op jit(solution)/shard_map/ppermute | solution.py:296
  6.6 3.5 %collective-permute-start.1 = (f32[2,16,128]{2,1,0:T(8,128)S(1)}, f32[2,16,128]{2,1,0:T(8,128)S(1)}, u32[]{:S(2)}, u32[]{:S(2)}) collective-permute-start(f32[2,16,128]{2,1,0:T(8,128)S(1)} %get-tuple-element.19), channel_id=1, source_target_pairs={{0,4},{1,2},{2,1},{3,7},{4,0},{5,6},{6,5},{7,3},{8,12},{9,10},{10,... | collective-permute-start | bytes 49160 | tf_op jit(solution)/shard_map/ppermute | solution.py:296
  6.6 5.2 %collective-permute-start.3 = (f32[16,128]{1,0:T(8,128)S(1)}, f32[16,128]{1,0:T(8,128)S(1)}, u32[]{:S(2)}, u32[]{:S(2)}) collective-permute-start(f32[16,128]{1,0:T(8,128)S(1)} %get-tuple-element.22), channel_id=1, source_target_pairs={{0,4},{4,0},{8,12},{12,8},{1,5},{5,1},{9,13},{13,9},{2,6},{6,2},{1... | collective-permute-start | bytes 24584 | tf_op jit(solution)/shard_map/ppermute | solution.py:296
  7.1 4.7 %collective-permute-start.4 = (f32[16,128]{1,0:T(8,128)S(1)}, f32[16,128]{1,0:T(8,128)S(1)}, u32[]{:S(2)}, u32[]{:S(2)}) collective-permute-start(f32[16,128]{1,0:T(8,128)S(1)} %get-tuple-element.23), channel_id=1, source_target_pairs={{0,12},{4,8},{8,4},{12,0},{1,13},{5,9},{9,5},{13,1},{2,14},{6,10},... | collective-permute-start | bytes 24584 | tf_op jit(solution)/shard_map/ppermute | solution.py:296
  13.3 6.4 %collective-permute-start.6 = (f32[4,64,128]{2,1,0:T(8,128)S(1)}, f32[4,64,128]{2,1,0:T(8,128)S(1)}, u32[]{:S(2)}, u32[]{:S(2)}) collective-permute-start(f32[4,64,128]{2,1,0:T(8,128)S(1)} %get-tuple-element.26), channel_id=1, source_target_pairs={{0,16},{16,0},{1,17},{17,1},{2,18},{18,2},{3,19},{19,3},{4,20},{20... | collective-permute-start | bytes 393224 | tf_op jit(solution)/shard_map/ppermute | solution.py:296
  13.9 8.2 %collective-permute-start.5 = (f32[4,64,128]{2,1,0:T(8,128)S(1)}, f32[4,64,128]{2,1,0:T(8,128)S(1)}, u32[]{:S(2)}, u32[]{:S(2)}) collective-permute-start(f32[4,64,128]{2,1,0:T(8,128)S(1)} %get-tuple-element.25), channel_id=1, source_target_pairs={{0,16},{16,0},{1,17},{17,1},{2,18},{18,2},{3,19},{19,3},{4,20},{20... | collective-permute-start | bytes 393224 | tf_op jit(solution)/shard_map/ppermute | solution.py:296

commit v3 on v2

--- a/solution.py
+++ b/solution.py
@@ -19,7 +19,6 @@
 ANY = pl.BlockSpec(memory_space=pl.ANY)
 VMEM = pl.BlockSpec(memory_space=pltpu.VMEM)
 ROOM = pltpu.CompilerParams(vmem_limit_bytes=8 << 20)
-SMEM = pl.BlockSpec(memory_space=pltpu.SMEM)
 
 
 def in_vmem(array):
@@ -60,8 +59,11 @@
     return (axis, first), ((beside, axis), second)
 
 
-def pack_kernel(volume, padded, cols, col_a, col_b, row_a, row_b, *rest):
-    *depth, packed, turned, sems = rest
+def pack_kernel(step_len, volume, *rest):
+    consts, rest = rest[:4], rest[4:]
+    table, padded, cols, col_a, col_b, row_a, row_b, *rest = rest
+    *depth, packed, turned = rest[:-6]
+    scalars, (sems, const_sems) = rest[-6:-2], rest[-2:]
     slices, rows, lanes = volume.shape
 
     group = slices // sems.shape[0]
@@ -74,6 +76,12 @@
 
     for g in range(sems.shape[0]):
         copy(g).start()
+    loads = [pltpu.make_async_copy(*each) for each in zip(consts, scalars, [const_sems.at[i] for i in range(4)])]
+    for load in loads:
+        load.start()
+    for load in loads:
+        load.wait()
+    fill_table(scalars, table, step_len)
     lane = lax.broadcasted_iota(jnp.int32, (rows, lanes), 1)
     packed[...] = jnp.zeros_like(packed)
     for s in range(slices):
@@ -99,42 +107,47 @@
         ref[...] = face
 
 
-def constants(consts, tile, step_len):
-    centers, widths, density, _ = consts
-    log2e = math.log2(math.e)
+def fill_table(scalars, table, step_len):
+    centers, widths, density, colors = scalars
+    tile = table.shape[1:]
+    terms = centers.shape[0]
 
     def splat(x):
         return jnp.full(tile, x, jnp.float32)
 
-    terms = range(centers.shape[0])
-    beta = [splat(-log2e) / (splat(widths[k]) * splat(widths[k])) for k in terms]
-    thick = [splat(density[k]) * (-log2e * step_len) for k in terms]
-    return [splat(centers[k]) for k in terms], beta, thick
-
-
-def transfer(current, centre, beta, thick):
+    for k in range(terms):
+        table[k] = splat(centers[k])
+        table[terms + k] = splat(-math.log2(math.e)) / (splat(widths[k]) * splat(widths[k]))
+        if k == 0:
+            table[2 * terms] = splat(density[0]) * (-math.log2(math.e) * step_len)
+        else:
+            table[2 * terms + k] = splat(density[k]) / splat(density[0])
+        for c in range(3):
+            table[(3 + c) * terms + k] = splat(colors[c, k]) * ((1 - AMBIENT) * LIGHT_Z)
+
+
+def transfer(current, table):
+    terms = table.shape[0] // 6
     bumps = []
-    for k in range(len(beta)):
-        off = current - centre[k]
-        bumps.append(jnp.exp2(off * beta[k] * off))
-    extinct, weight = thick[0] * bumps[0], bumps[0] + 1.0
-    for k in range(1, len(beta)):
-        extinct = extinct + thick[k] * bumps[k]
+    for k in range(terms):
+        off = current - table[k]
+        bumps.append(jnp.exp2(off * table[terms + k] * off))
+    extinct, weight = bumps[0], bumps[0] + 1.0
+    for k in range(1, terms):
+        extinct = extinct + table[2 * terms + k] * bumps[k]
         weight = weight + bumps[k]
     return bumps, extinct, weight
 
 
-def prepare(padded, consts, pre, first_row, step_len):
-    count, slices, rows, lanes = pre.shape
-    tile = (8, lanes)
-    values = constants(consts, tile, step_len)
+def prepare(padded, table, pre, first_row):
+    count, slices, rows, _ = pre.shape
 
     def chunk(index, _):
         for j in range(ROWS_AT_ONCE):
             at = pl.multiple_of((index * ROWS_AT_ONCE + j) * 8, 8)
             row = pl.multiple_of(first_row + at, 8)
             for s in range(slices):
-                bumps, extinct, weight = transfer(padded[s, pl.ds(row + PAD, 8), :], *values)
+                bumps, extinct, weight = transfer(padded[s, pl.ds(row + PAD, 8), :], table)
                 share = 1.0 / weight
                 for k in range(count - 1):
                     pre[k, s, pl.ds(at, 8), :] = bumps[k] * share
@@ -144,13 +157,13 @@
     lax.fori_loop(0, rows // (8 * ROWS_AT_ONCE), chunk, 0)
 
 
-def render(padded, edges, below, above, consts, outs, first_row, step_len, pre=None, pre_row=0):
-    colors = consts[3]
+def render(padded, edges, below, above, table, outs, first_row, pre=None):
     slices, _, lanes = padded.shape
     rows = outs.shape[1]
-    terms = colors.shape[1]
+    terms = table.shape[0] // 6
     tile = (8, lanes)
-    values = constants(consts, tile, step_len) if pre is None else None
+    thick = table[2 * terms]
+    thick_lit = thick * 3.2
     lane = lax.broadcasted_iota(jnp.int32, tile, 1)
     edge = (lane == 0) | (lane == lanes - 1)
     zero, one = jnp.zeros(tile, jnp.float32), jnp.ones(tile, jnp.float32)
@@ -159,7 +172,6 @@
         for j in range(ROWS_AT_ONCE):
             at = pl.multiple_of((index * ROWS_AT_ONCE + j) * 8, 8)
             row = pl.multiple_of(first_row + at, 8)
-            pre_at = pl.multiple_of(pre_row + at, 8)
             edge_rows = edges[pl.ds(row, 8), :]
             total, trans = [zero] * terms, one
             before = below(row)
@@ -174,21 +186,21 @@
                 lit = jnp.abs(dx * (LIGHT_X / LIGHT_Z) + dy * (LIGHT_Y / LIGHT_Z) + dz)
                 shade = lit * inv + AMBIENT / ((1 - AMBIENT) * LIGHT_Z)
                 if pre is None:
-                    bumps, extinct, weight = transfer(current, *values)
+                    bumps, extinct, weight = transfer(current, table)
                     shade = shade / weight
                 else:
-                    bumps = [pre[k, s, pl.ds(pre_at, 8), :] for k in range(terms)]
-                    extinct = pre[terms, s, pl.ds(pre_at, 8), :]
-                passed = jnp.exp2(extinct * (1.0 - 3.2 * (inv * inv)))
+                    bumps = [pre[k, s, pl.ds(at, 8), :] for k in range(terms)]
+                    extinct = pre[terms, s, pl.ds(at, 8), :]
+                passed = jnp.exp2(extinct * (thick - thick_lit * (inv * inv)))
                 left = trans * passed
                 amount = (trans - left) * shade
                 total = [total[k] + amount * bumps[k] for k in range(terms)]
                 trans = left
                 before, current = current, after
             for c in range(3):
-                mixed = total[0] * (colors[c, 0] * ((1 - AMBIENT) * LIGHT_Z))
+                mixed = total[0] * table[(3 + c) * terms]
                 for k in range(1, terms):
-                    mixed = mixed + total[k] * (colors[c, k] * ((1 - AMBIENT) * LIGHT_Z))
+                    mixed = mixed + total[k] * table[(3 + c) * terms + k]
                 outs[c, pl.ds(at, 8), :] = mixed
             outs[3, pl.ds(at, 8), :] = trans
         return 0
@@ -230,41 +242,37 @@
 def partner_rows(rows, inner):
     ahead = lax.axis_index("depth") == 0
     quarter = rows // 4
-    at = jnp.where(ahead == inner, 0, quarter)
-    return pl.multiple_of(jnp.where(ahead, 2 * quarter, 0) + at, 8), pl.multiple_of(at, 8)
-
-
-def before_kernel(step_len, centers, widths, density, colors, padded, pre):
-    rows = 2 * pre.shape[2]
-    start = pl.multiple_of((1 - lax.axis_index("depth")) * (rows // 2), 8)
-    prepare(padded, (centers, widths, density, colors), pre, start, step_len)
-
-
-def inner_kernel(step_len, centers, widths, density, colors, padded, pre, cols, col_a, col_b, depth_a, edges, outs, turned):
+    return pl.multiple_of(jnp.where(ahead, 2 * quarter, 0) + jnp.where(ahead == inner, 0, quarter), 8)
+
+
+def before_kernel(table, padded, pre):
+    rows = 4 * pre.shape[2]
+    prepare(padded, table, pre, partner_rows(rows, True))
+
+
+def inner_kernel(table, padded, pre, cols, col_a, col_b, depth_a, edges, outs, turned):
     turn_edges(cols, col_a, col_b, edges, turned)
     below, above = depth_faces(depth_a, depth_a)
-    row, pre_row = partner_rows(edges.shape[0], True)
-    render(padded, edges, below, above, (centers, widths, density, colors), outs, row, step_len, pre, pre_row)
-
-
-def outer_kernel(step_len, centers, widths, density, colors, padded, pre, edges, row_a, row_b, depth_a, full, outs):
+    render(padded, edges, below, above, table, outs, partner_rows(edges.shape[0], True), pre)
+
+
+def outer_kernel(table, padded, edges, row_a, row_b, depth_a, full, outs):
     fill_rows(row_a, row_b, full)
     below, above = depth_faces(depth_a, depth_a)
-    row, pre_row = partner_rows(edges.shape[0], False)
-    render(full, edges, below, above, (centers, widths, density, colors), outs, row, step_len, pre, pre_row)
-
-
-def own_kernel(step_len, centers, widths, density, colors, full, edges, depth_a, outs):
+    render(full, edges, below, above, table, outs, partner_rows(edges.shape[0], False))
+
+
+def own_kernel(table, full, edges, depth_a, outs):
     below, above = depth_faces(depth_a, depth_a)
     row = pl.multiple_of(lax.axis_index("depth") * outs.shape[1], 8)
-    render(full, edges, below, above, (centers, widths, density, colors), outs, row, step_len)
-
-
-def whole_kernel(step_len, centers, widths, density, colors, padded, cols, col_a, col_b, row_a, row_b, depth_a, depth_b, full, outs, edges, turned):
+    render(full, edges, below, above, table, outs, row)
+
+
+def whole_kernel(table, padded, cols, col_a, col_b, row_a, row_b, depth_a, depth_b, full, outs, edges, turned):
     turn_edges(cols, col_a, col_b, edges, turned)
     fill_rows(row_a, row_b, full)
     below, above = depth_faces(depth_a, depth_b)
-    render(full, edges, below, above, (centers, widths, density, colors), outs, 0, step_len)
+    render(full, edges, below, above, table, outs, 0)
 
 
 def join_kernel(own, inner, outer, image):
@@ -308,17 +316,20 @@
     side = (rows // lanes, slices, lanes)
     turned = vmem_out(rows // lanes, lanes, lanes)
     image = jax.ShapeDtypeStruct((4, part, lanes), jnp.float32)
-    out_shape = (block, vmem_out(2, *side)) + (vmem_out(*side),) * 2 + (vmem_out(slices, lanes),) * 2 + (face,) * (1 if pair else 2)
-    padded, cols, col_a, col_b, row_a, row_b, *depth = pl.pallas_call(
-        pack_kernel,
+    terms = centers.shape[0]
+    out_shape = (vmem_out(6 * terms, 8, lanes), block, vmem_out(2, *side)) + (vmem_out(*side),) * 2 + (vmem_out(slices, lanes),) * 2 + (face,) * (1 if pair else 2)
+    table, padded, cols, col_a, col_b, row_a, row_b, *depth = pl.pallas_call(
+        functools.partial(pack_kernel, step_len),
         out_shape=out_shape,
-        in_specs=[ANY],
+        in_specs=[ANY] * 5,
         out_specs=(VMEM,) * len(out_shape),
-        scratch_shapes=[face, turned, pltpu.SemaphoreType.DMA((math.gcd(slices, LOADS),))],
+        scratch_shapes=[face, turned]
+        + [pltpu.SMEM(each.shape, jnp.float32) for each in consts]
+        + [pltpu.SemaphoreType.DMA((math.gcd(slices, LOADS),)), pltpu.SemaphoreType.DMA((4,))],
         compiler_params=ROOM,
         name="pack",
-    )(in_hbm(volume))
-    padded, cols = in_vmem(padded), in_vmem(cols)
+    )(in_hbm(volume), *consts)
+    table, padded, cols = in_vmem(table), in_vmem(padded), in_vmem(cols)
 
     depth = [swap(array, to) for array, to in zip(depth, swap_rounds("depth"))]
     col_a, col_b = (swap(array, to) for array, to in zip((col_a, col_b), swap_rounds("ty", "tx")))
@@ -328,14 +339,14 @@
 
     def call(kernel, out_shape, args, scratch=(), aliases={}):
         return pl.pallas_call(
-            functools.partial(kernel, step_len),
+            kernel,
             out_shape=out_shape,
-            in_specs=[SMEM] * 4 + [VMEM] * len(args),
+            in_specs=[VMEM] * (1 + len(args)),
             out_specs=jax.tree.map(lambda _: VMEM, out_shape),
             scratch_shapes=scratch,
             input_output_aliases=aliases,
             compiler_params=ROOM,
-        )(*consts, *args)
+        )(table, *args)
 
     if not pair:
         _, sent = call(
@@ -343,21 +354,21 @@
             (block, vmem_out(4, rows, lanes)),
             (padded, cols, col_a, col_b, row_a, row_b, *depth),
             [face, turned],
-            {4: 0},
+            {1: 0},
         )
         parts = jnp.swapaxes(sent.reshape(4, depth_count, part, lanes), 0, 1)
         parts = lax.all_to_all(parts, "depth", 0, 0)
         return pl.pallas_call(chain_kernel, out_shape=image, compiler_params=ROOM, name="chain")(parts)
 
     both = ("depth", [(0, 1), (1, 0)])
-    pre = in_vmem(call(before_kernel, vmem_out(colors.shape[1] + 1, slices, part, lanes), (padded,)))
+    pre = in_vmem(call(before_kernel, vmem_out(terms + 1, slices, part // 2, lanes), (padded,)))
     edges, inner = call(
         inner_kernel, (face, vmem_out(4, part // 2, lanes)), (padded, pre, cols, col_a, col_b, *depth), [turned]
     )
     edges = in_vmem(edges)
     other_inner = swap(inner, both)
     full, outer = call(
-        outer_kernel, (block, vmem_out(4, part // 2, lanes)), (padded, pre, edges, row_a, row_b, *depth), aliases={4: 0}
+        outer_kernel, (block, vmem_out(4, part // 2, lanes)), (padded, edges, row_a, row_b, *depth), aliases={1: 0}
     )
     other_outer = swap(outer, both)
     own = call(own_kernel, vmem_out(4, part, lanes), (in_vmem(full), edges, *depth))

time: 23.1 us -> 20.6 us (0.89)
  Pallas kernels: 10.8 us -> 7.63 us
  waiting for transfers between devices: 3.59 us -> 4.45 us
    pallas_call x5, Pallas kernels: 10.1 us -> 6.89 us  [the longest x4 4.9 us: call(): pl.pallas_call(kernel, out_shape=out_shape, in_specs=[VMEM] * (1 + len(ar...]
    ppermute x7, waiting for transfers between devices: 3.59 us -> 4.45 us  [swap(): return in_vmem(lax.ppermute(array, axes, pairs))]
  transfers between devices with their start and end apart: 7 -> 7, of which waited for: 2 -> 3; matrix products, arithmetic and copies ran while one was open for 0% -> 0% of each run, Pallas kernels for 29% -> 18%
where the time goes in v3:
time: 20.6 us; the launch traced here: 20.5 us
  starting transfers between devices  8.34 us (40%)
  Pallas kernels  7.63 us (37%)
  waiting for transfers between devices  4.45 us (22%)
    ppermute x7, starting transfers between devices, swap(): return in_vmem(lax.ppermute(array, axes, pairs))  8.34 us
    pallas_call x4, Pallas kernels, call(): pl.pallas_call(kernel, out_shape=out_shape, in_specs=[VMEM] * (1 + len(ar...  4.9 us
    ppermute x7, waiting for transfers between devices, swap(): return in_vmem(lax.ppermute(array, axes, pairs))  4.45 us
    pallas_call x1, Pallas kernels, on_device(): pl.pallas_call(functools.partial(pack_kernel, step_len), out_shape=out_sh...  1.99 us
    pallas_call x1, Pallas kernels, on_device(): pl.pallas_call(join_kernel, out_shape=image, in_specs=[VMEM] * 3, out_spe...  0.74 us
  transfers between devices with their start and end apart: 7, of which 3 were waited for; matrix products, arithmetic and copies ran while one was open for 0% of the time, Pallas kernels for 18%

profile of v3, /device:TPU:0, one launch (start us, length us, event | category | flops | bytes accessed | tf_op | source)
XLA Modules:
  0.0 20.5 jit_solution(15868053167736688764)
XLA Ops:
  0.0 2.0 %pack.1 = (f32[24,8,128]{2,1,0:T(8,128)S(1)}, f32[16,272,128]{2,1,0:T(8,128)S(1)}, f32[2,2,16,128]{3,2,1,0:T(8,128)S(1)}, f32[2,16,128]{2,1,0:T(8,128)S(1)}, f32...) custom-call(f32[16,256,128]{2,1,0:T(8,128)} %volume.1, ...), custom_call_target="tpu_custom_call" | custom-call | tf_op jit(solution)/shard_map/pack/pallas_call | solution.py:321
  2.0 3.0 %collective-permute-start.2 = (f32[256,128]{1,0:T(8,128)S(1)}, f32[256,128]{1,0:T(8,128)S(1)}, u32[]{:S(2)}, u32[]{:S(2)}) collective-permute-start(f32[256,128]{1,0:T(8,128)S(1)} %get-tuple-element.22), channel_id=1, source_target_pairs={{0,16},{16,0},{1,17},{17,1},{2,18},{18,2},{3,19},{19,3},{4,20},{20... | collective-permute-start | bytes 393224 | tf_op jit(solution)/shard_map/ppermute | solution.py:304
  5.0 1.6 %collective-permute-start = (f32[2,16,128]{2,1,0:T(8,128)S(1)}, f32[2,16,128]{2,1,0:T(8,128)S(1)}, u32[]{:S(2)}, u32[]{:S(2)}) collective-permute-start(f32[2,16,128]{2,1,0:T(8,128)S(1)} %get-tuple-element.20), channel_id=1, source_target_pairs={{0,1},{1,0},{2,3},{3,2},{4,5},{5,4},{6,7},{7,6},{8,9},{9,8},{10,11... | collective-permute-start | bytes 49160 | tf_op jit(solution)/shard_map/ppermute | solution.py:304
  6.6 0.0 collective-permute-start.1
  6.6 0.5 %collective-permute-start.3 = (f32[16,128]{1,0:T(8,128)S(1)}, f32[16,128]{1,0:T(8,128)S(1)}, u32[]{:S(2)}, u32[]{:S(2)}) collective-permute-start(f32[16,128]{1,0:T(8,128)S(1)} %get-tuple-element.24), channel_id=1, source_target_pairs={{0,4},{4,0},{8,12},{12,8},{1,5},{5,1},{9,13},{13,9},{2,6},{6,2},{1... | collective-permute-start | bytes 24584 | tf_op jit(solution)/shard_map/ppermute | solution.py:304
  7.1 1.1 %collective-permute-start.4 = (f32[16,128]{1,0:T(8,128)S(1)}, f32[16,128]{1,0:T(8,128)S(1)}, u32[]{:S(2)}, u32[]{:S(2)}) collective-permute-start(f32[16,128]{1,0:T(8,128)S(1)} %get-tuple-element.25), channel_id=1, source_target_pairs={{0,12},{4,8},{8,4},{12,0},{1,13},{5,9},{9,5},{13,1},{2,14},{6,10},... | collective-permute-start | bytes 24584 | tf_op jit(solution)/shard_map/ppermute | solution.py:304
  8.2 0.6 %shard_map.55.pre = f32[5,16,64,128]{3,2,1,0:T(8,128)S(1)} custom-call(f32[24,8,128]{2,1,0:T(8,128)S(1)} %get-tuple-element.17.table, f32[16,272,128]{2,1,0:T(8,128)S(1)} %get-tuple-element.18.padded), custom_call_target="tpu_custom_call" | custom-call | tf_op jit(solution)/shard_map/pallas_call | solution.py:341
  8.8 0.0 collective-permute-done.col_a
  8.8 0.0 collective-permute-done.1.col_b
  8.8 0.0 collective-permute-done.2.depth_a
  8.8 0.9 %shard_map.56 = (f32[256,128]{1,0:T(8,128)S(1)}, f32[4,64,128]{2,1,0:T(8,128)S(1)}) custom-call(f32[24,8,128]{2,1,0:T(8,128)S(1)} %get-tuple-element.17.table, f32[16,272,128]{2,1,0:T(8,128)S(1)} %get-tuple-element.18.padded, f32[5,16,64,128]{3,2,1,0:T(8,128)S(1)} %shard_map.55.pre, f32[2,2,16,128]{3,2,1,0:T(8,128)S(1)} %get-tuple-element.19.cols, ...), custom_call_target="tpu_custom_call" | custom-call | tf_op jit(solution)/shard_map/pallas_call | solution.py:341
  9.8 0.0 collective-permute-done.3.row_a
  9.8 0.4 %collective-permute-done.4.row_b = f32[16,128]{1,0:T(8,128)S(1)} collective-permute-done((f32[16,128]{1,0:T(8,128)S(1)}, f32[16,128]{1,0:T(8,128)S(1)}, u32[]{:S(2)}, u32[]{:S(2)}) %collective-permute-start.4) | collective-permute-done | bytes 8224 | tf_op jit(solution)/shard_map/ppermute | solution.py:304
  10.2 1.2 %shard_map.57 = (f32[16,272,128]{2,1,0:T(8,128)S(1)}, f32[4,64,128]{2,1,0:T(8,128)S(1)}) custom-call(f32[24,8,128]{2,1,0:T(8,128)S(1)} %get-tuple-element.17.table, f32[16,272,128]{2,1,0:T(8,128)S(1)} %get-tuple-element.18.padded, f32[256,128]{1,0:T(8,128)S(1)} %get-tuple-element.23.edges, ...), custom_call_target="tpu_custom_call", output_to_operand_aliasing={{0}: (1, {})} | custom-call | tf_op jit(solution)/shard_map/pallas_call | solution.py:341
  11.4 1.1 %collective-permute-start.6 = (f32[4,64,128]{2,1,0:T(8,128)S(1)}, f32[4,64,128]{2,1,0:T(8,128)S(1)}, u32[]{:S(2)}, u32[]{:S(2)}) collective-permute-start(f32[4,64,128]{2,1,0:T(8,128)S(1)} %get-tuple-element.28), channel_id=1, source_target_pairs={{0,16},{16,0},{1,17},{17,1},{2,18},{18,2},{3,19},{19,3},{4,20},{20... | collective-permute-start | bytes 393224 | tf_op jit(solution)/shard_map/ppermute | solution.py:304
  12.4 1.0 %collective-permute-start.5 = (f32[4,64,128]{2,1,0:T(8,128)S(1)}, f32[4,64,128]{2,1,0:T(8,128)S(1)}, u32[]{:S(2)}, u32[]{:S(2)}) collective-permute-start(f32[4,64,128]{2,1,0:T(8,128)S(1)} %get-tuple-element.27), channel_id=1, source_target_pairs={{0,16},{16,0},{1,17},{17,1},{2,18},{18,2},{3,19},{19,3},{4,20},{20... | collective-permute-start | bytes 393224 | tf_op jit(solution)/shard_map/ppermute | solution.py:304
  13.5 2.3 %shard_map.58.own = f32[4,128,128]{2,1,0:T(8,128)S(1)} custom-call(f32[24,8,128]{2,1,0:T(8,128)S(1)} %get-tuple-element.17.table, f32[16,272,128]{2,1,0:T(8,128)S(1)} %get-tuple-element.26.full, f32[256,128]{1,0:T(8,128)S(1)} %get-tuple-element.23.edges, f32[256,128]{1,0:T(8,128)S(1)} %collective-permute-done.2.depth_a), custom_call_target="tpu_custom_call" | custom-call | tf_op jit(solution)/shard_map/pallas_call | solution.py:341
  15.7 2.1 %collective-permute-done.6.outer = f32[4,64,128]{2,1,0:T(8,128)S(1)} collective-permute-done((f32[4,64,128]{2,1,0:T(8,128)S(1)}, f32[4,64,128]{2,1,0:T(8,128)S(1)}, u32[]{:S(2)}, u32[]{:S(2)}) %collective-permute-start.6) | collective-permute-done | bytes 131104 | tf_op jit(solution)/shard_map/ppermute | solution.py:304
  17.8 2.0 %collective-permute-done.5.inner = f32[4,64,128]{2,1,0:T(8,128)S(1)} collective-permute-done((f32[4,64,128]{2,1,0:T(8,128)S(1)}, f32[4,64,128]{2,1,0:T(8,128)S(1)}, u32[]{:S(2)}, u32[]{:S(2)}) %collective-permute-start.5) | collective-permute-done | bytes 131104 | tf_op jit(solution)/shard_map/ppermute | solution.py:304
  19.8 0.7 %join.1 = f32[4,128,128]{2,1,0:T(8,128)} custom-call(f32[4,128,128]{2,1,0:T(8,128)S(1)} %shard_map.58.own, f32[4,64,128]{2,1,0:T(8,128)S(1)} %collective-permute-done.5.inner, f32[4,64,128]{2,1,0:T(8,128)S(1)} %collective-permute-done.6.outer), custom_call_target="tpu_custom_call" | custom-call | tf_op jit(solution)/shard_map/join/pallas_call | solution.py:375
Async XLA Ops:
  2.0 6.8 %collective-permute-start.2 = (f32[256,128]{1,0:T(8,128)S(1)}, f32[256,128]{1,0:T(8,128)S(1)}, u32[]{:S(2)}, u32[]{:S(2)}) collective-permute-start(f32[256,128]{1,0:T(8,128)S(1)} %get-tuple-element.22), channel_id=1, source_target_pairs={{0,16},{16,0},{1,17},{17,1},{2,18},{18,2},{3,19},{19,3},{4,20},{20... | collective-permute-start | bytes 393224 | tf_op jit(solution)/shard_map/ppermute | solution.py:304
  5.0 3.8 %collective-permute-start = (f32[2,16,128]{2,1,0:T(8,128)S(1)}, f32[2,16,128]{2,1,0:T(8,128)S(1)}, u32[]{:S(2)}, u32[]{:S(2)}) collective-permute-start(f32[2,16,128]{2,1,0:T(8,128)S(1)} %get-tuple-element.20), channel_id=1, source_target_pairs={{0,1},{1,0},{2,3},{3,2},{4,5},{5,4},{6,7},{7,6},{8,9},{9,8},{10,11... | collective-permute-start | bytes 49160 | tf_op jit(solution)/shard_map/ppermute | solution.py:304
  6.6 2.2 %collective-permute-start.1 = (f32[2,16,128]{2,1,0:T(8,128)S(1)}, f32[2,16,128]{2,1,0:T(8,128)S(1)}, u32[]{:S(2)}, u32[]{:S(2)}) collective-permute-start(f32[2,16,128]{2,1,0:T(8,128)S(1)} %get-tuple-element.21), channel_id=1, source_target_pairs={{0,4},{1,2},{2,1},{3,7},{4,0},{5,6},{6,5},{7,3},{8,12},{9,10},{10,... | collective-permute-start | bytes 49160 | tf_op jit(solution)/shard_map/ppermute | solution.py:304
  6.6 3.1 %collective-permute-start.3 = (f32[16,128]{1,0:T(8,128)S(1)}, f32[16,128]{1,0:T(8,128)S(1)}, u32[]{:S(2)}, u32[]{:S(2)}) collective-permute-start(f32[16,128]{1,0:T(8,128)S(1)} %get-tuple-element.24), channel_id=1, source_target_pairs={{0,4},{4,0},{8,12},{12,8},{1,5},{5,1},{9,13},{13,9},{2,6},{6,2},{1... | collective-permute-start | bytes 24584 | tf_op jit(solution)/shard_map/ppermute | solution.py:304
  7.1 3.1 %collective-permute-start.4 = (f32[16,128]{1,0:T(8,128)S(1)}, f32[16,128]{1,0:T(8,128)S(1)}, u32[]{:S(2)}, u32[]{:S(2)}) collective-permute-start(f32[16,128]{1,0:T(8,128)S(1)} %get-tuple-element.25), channel_id=1, source_target_pairs={{0,12},{4,8},{8,4},{12,0},{1,13},{5,9},{9,5},{13,1},{2,14},{6,10},... | collective-permute-start | bytes 24584 | tf_op jit(solution)/shard_map/ppermute | solution.py:304
  11.4 6.4 %collective-permute-start.6 = (f32[4,64,128]{2,1,0:T(8,128)S(1)}, f32[4,64,128]{2,1,0:T(8,128)S(1)}, u32[]{:S(2)}, u32[]{:S(2)}) collective-permute-start(f32[4,64,128]{2,1,0:T(8,128)S(1)} %get-tuple-element.28), channel_id=1, source_target_pairs={{0,16},{16,0},{1,17},{17,1},{2,18},{18,2},{3,19},{19,3},{4,20},{20... | collective-permute-start | bytes 393224 | tf_op jit(solution)/shard_map/ppermute | solution.py:304
  12.4 7.3 %collective-permute-start.5 = (f32[4,64,128]{2,1,0:T(8,128)S(1)}, f32[4,64,128]{2,1,0:T(8,128)S(1)}, u32[]{:S(2)}, u32[]{:S(2)}) collective-permute-start(f32[4,64,128]{2,1,0:T(8,128)S(1)} %get-tuple-element.27), channel_id=1, source_target_pairs={{0,16},{16,0},{1,17},{17,1},{2,18},{18,2},{3,19},{19,3},{4,20},{20... | collective-permute-start | bytes 393224 | tf_op jit(solution)/shard_map/ppermute | solution.py:304
